TPU v7x, 512 devices: a whole 4x8x8 slice. The times are simulated.
512 devices in a mesh: dom: 32 (over z, x), group: 16 (over y, core).
Axes of the slice: x: 4, y: 8, z: 8, core: 2. Of those that a mesh axis runs over, the one named last changes fastest.
Arguments:
- features: bfloat16 [1048576, 256], P(('dom', 'group')), may hold values from -6 to 6
- boundary: int32 [8192], P(('dom', 'group')), may hold values from 0 to 127, as said below
- request: int32 [8192, 6], P(('dom', 'group')), may hold values from 0 to 15, as said below
- tile_slots: int32 [8192, 8], P(('dom', 'group')), may hold values from 0 to 223, as said below
- neighbors: int32 [1048576, 10], P(('dom', 'group')), may hold values from 0 to 127
- negatives: int32 [1048576, 4], P(('dom', 'group')), may hold values from 0 to 127
- layer_weight: bfloat16 [512, 256], replicated, may hold values from -0.25 to 0.25
Outputs:
- feature_grad: float32 [1048576, 256], P(('dom', 'group'))
- weight_grad: float32 [512, 256], replicated
- loss_mean: float32 [], replicated
Inputs may be any that keep to these rules, and one draw needn't show every extreme that they name: The 16 entries boundary[i * 16 to i * 16 + 15] are distinct numbers of device i's own row blocks. `request`: row i * 16 + e holds 6 distinct positions in the boundary list of device (i // 16) * 16 + e. `tile_slots`: entries are numbers s as in the first step; the 128 entries of one device are distinct and include every number from 128 to 223.
All inputs are finite; a program needn't handle non-finite values.
Results may differ from a plain program's by a relative error of at most 0.00075.
The roundings to bfloat16 on the way count: a program that leaves them out, or rounds other values in their place, can miss the bound.
Values may be sent and summed in bfloat16 or wider, within the bound.
A program may use at most 64 MiB of HBM per device.

v0:
```python
import jax
import jax.numpy as jnp
from jax import lax
from jax.sharding import Mesh
from jax.sharding import PartitionSpec as P

TILE = 128
BLK = 16
NBT = 8
DEG = 10
NNEG = 4
GROUP = ("group_0", "group_1")
DOM_GROUP = ("dom_0", "dom_1", "group_0", "group_1")


margin = 0.5
epsilon = 1e-06


def cut_along(array, dim, length):
    before, after = (array.shape[:dim], array.shape[dim + 1 :])
    return jnp.moveaxis(array.reshape(*before, length, -1, *after), dim, 0)


def sent_and_summed(array, axis, dim):
    length = lax.axis_size(axis)
    tiles = lax.all_to_all(cut_along(array, dim, length), axis, 0, 0, tiled=True)
    return jnp.sum(tiles, axis=0)


def sum_by_axis(array, axes, dim):
    far, near = axes
    own = sent_and_summed(cut_along(array, dim, lax.axis_size(far)), near, dim + 1)
    return jnp.sum(lax.all_to_all(own, far, 0, 0, tiled=True), axis=0)


def padded_to(lines, length):
    spare = -lines.shape[0] % length
    if not spare:
        return lines
    return jnp.concatenate([lines, jnp.zeros((spare, *lines.shape[1:]), lines.dtype)])


def from_everyone(array, axis):
    copies = jnp.broadcast_to(array, (lax.axis_size(axis), *array.shape))
    return lax.all_to_all(copies, axis, split_axis=0, concat_axis=0, tiled=True)


def in_order(tiles, dim):
    shape = list(tiles.shape[1:])
    shape[dim] *= tiles.shape[0]
    return jnp.moveaxis(tiles, 0, dim).reshape(shape)


def gathered_by_axis(array, axes, dim):
    far, near = axes
    leading = from_everyone(array, far)
    tiles = jnp.swapaxes(from_everyone(leading, near), 0, 1)
    return in_order(tiles.reshape(-1, *array.shape), dim)


def total_of(array, axes):
    own = sum_by_axis(padded_to(array, lax.axis_size(axes[0]) * lax.axis_size(axes[1])), axes, 0)
    whole = gathered_by_axis(own, axes, 0)
    return whole[: len(array)].reshape(array.shape)


def together(arrays, axis):
    ends = [0]
    for a in arrays:
        ends.append(ends[-1] + a.size)
    total = total_of(jnp.concatenate([a.ravel() for a in arrays]), axis)
    return tuple((total[b:e].reshape(a.shape) for a, b, e in zip(arrays, ends, ends[1:])))


def contract(form, left, right):
    return jnp.einsum(form, left, right, preferred_element_type=jnp.float32)


def tile_terms(own_rows, candidates, neighbor_ids, negative_ids, layer_weight):
    tile_count, tile_rows, feature_width = own_rows.shape
    cand_count = candidates.shape[1]
    degree = neighbor_ids.shape[-1]
    negative_count = negative_ids.shape[-1]
    slot_ids = jnp.arange(cand_count, dtype=jnp.int32)
    counts = jnp.sum((neighbor_ids[..., None] == slot_ids).astype(jnp.float32), axis=2).astype(
        jnp.bfloat16
    )
    aggregate = (contract("tuc,tcd->tud", counts, candidates) / degree).astype(jnp.bfloat16)
    joined = jnp.concatenate([own_rows, aggregate], axis=-1).reshape(-1, 2 * feature_width)
    preact = jnp.dot(joined, layer_weight, preferred_element_type=jnp.float32)
    gate_value = jax.nn.sigmoid(preact)
    hidden = preact * gate_value
    norm_scale = lax.rsqrt(jnp.mean(hidden * hidden, axis=-1, keepdims=True) + epsilon)
    embedding = hidden * norm_scale
    embed_half = embedding.astype(jnp.bfloat16).reshape(tile_count, tile_rows, feature_width)
    inv_root = feature_width ** (-0.5)
    scores = contract("tud,tcd->tuc", embed_half, candidates) * inv_root
    positive = (neighbor_ids[..., 0:1] == slot_ids).astype(jnp.float32)
    negative = (negative_ids[..., None] == slot_ids).astype(jnp.float32)
    pos_score = jnp.sum(scores * positive, axis=-1, keepdims=True)
    neg_score = jnp.sum(scores[:, :, None, :] * negative, axis=-1)
    excess = margin + neg_score - pos_score
    loss_sum = jnp.sum(jax.nn.softplus(excess)) / negative_count
    neg_weight = jax.nn.sigmoid(excess) / negative_count
    dscores = (
        jnp.sum(neg_weight[..., None] * negative, axis=2)
        - jnp.sum(neg_weight, axis=-1, keepdims=True) * positive
    ) * inv_root
    dscores_half = dscores.astype(jnp.bfloat16)
    dembedding = contract("tuc,tcd->tud", dscores_half, candidates).reshape(-1, feature_width)
    dcandidates = contract("tuc,tud->tcd", dscores_half, embed_half)
    dhidden = norm_scale * (
        dembedding - embedding * jnp.mean(dembedding * embedding, axis=-1, keepdims=True)
    )
    dpreact = (dhidden * gate_value * (1.0 + preact * (1.0 - gate_value))).astype(jnp.bfloat16)
    dweight = jnp.dot(joined.T, dpreact, preferred_element_type=jnp.float32)
    dinputs = jnp.dot(dpreact, layer_weight.T, preferred_element_type=jnp.float32)
    dself = dinputs[:, :feature_width].reshape(tile_count, tile_rows, feature_width)
    daggregate = (
        (dinputs[:, feature_width:] / degree)
        .astype(jnp.bfloat16)
        .reshape(tile_count, tile_rows, feature_width)
    )
    dcandidates = dcandidates + contract("tuc,tud->tcd", counts, daggregate)
    return (loss_sum, dweight, dself, dcandidates)


def per_device(features, boundary, request, tile_slots, neighbors, negatives, layer_weight):
    row_count, feature_width = features.shape
    peer_count = lax.axis_size(GROUP)
    capacity = request.shape[1]
    bound_count = boundary.shape[0]
    block_count = row_count // BLK
    tile_count = tile_slots.shape[0]
    blocks = features.reshape(block_count, BLK, feature_width)
    asked_for = lax.all_to_all(request, GROUP, split_axis=0, concat_axis=0, tiled=True)
    picked = jnp.sum(
        jnp.where(asked_for[..., None] == jnp.arange(bound_count, dtype=jnp.int32), boundary, 0),
        axis=-1,
    )
    outgoing = blocks[picked.reshape(-1)].reshape(peer_count, capacity * BLK, feature_width)
    received = lax.all_to_all(outgoing, GROUP, split_axis=0, concat_axis=0, tiled=True)
    table_rows = jnp.concatenate(
        [blocks, received.reshape(peer_count * capacity, BLK, feature_width)], axis=0
    )
    slot_list = tile_slots.reshape(-1)
    candidates = table_rows[slot_list].reshape(tile_count, NBT * BLK, feature_width)
    own_rows = features.reshape(tile_count, TILE, feature_width)
    neighbor_ids = neighbors.reshape(tile_count, TILE, DEG)
    negative_ids = negatives.reshape(tile_count, TILE, NNEG)
    loss_sum, dweight, dself, dcandidates = tile_terms(
        own_rows, candidates, neighbor_ids, negative_ids, layer_weight
    )
    table_grad = jnp.zeros((block_count + peer_count * capacity, BLK, feature_width), jnp.float32)
    table_grad = table_grad.at[slot_list].add(dcandidates.reshape(-1, BLK, feature_width))
    own_grad = table_grad[:block_count] + dself.reshape(block_count, BLK, feature_width)
    incoming = table_grad[block_count:]
    returned = lax.all_to_all(
        incoming.reshape(peer_count, capacity * BLK, feature_width),
        GROUP,
        split_axis=0,
        concat_axis=0,
        tiled=True,
    )
    own_grad = own_grad.at[picked.reshape(-1)].add(returned.reshape(-1, BLK, feature_width))
    totals = together((dweight, loss_sum), ("dom_0", ("dom_1", "group_0", "group_1")))
    device_total = lax.axis_size(DOM_GROUP)
    return (
        own_grad.reshape(row_count, feature_width),
        totals[0] / row_count,
        totals[1] / (row_count * device_total),
    )


def solution(mesh):
    finer = Mesh(mesh.devices.reshape(8, 4, 8, 2), ("dom_0", "dom_1", "group_0", "group_1"))
    return jax.shard_map(
        per_device,
        mesh=finer,
        in_specs=(
            P(DOM_GROUP, None),
            P(DOM_GROUP),
            P(DOM_GROUP, None),
            P(DOM_GROUP, None),
            P(DOM_GROUP, None),
            P(DOM_GROUP, None),
            P(),
        ),
        out_specs=(P(DOM_GROUP, None), P(), P()),
        check_vma=False,
    )
```

profile of v0, /device:TPU:1, one launch (start us, length us, event | category | flops | bytes accessed | tf_op | source)
XLA Modules:
  0.0 228.2 jit_solution(10251627791465795777)
XLA Ops:
  1.5 16.3 %all_to_all.47 = s32[16,1,6]{2,1,0:T(1,128)S(1)} all-to-all(s32[16,1,6]{2,1,0:T(1,128)S(1)} %copy.48), channel_id=1, replica_groups=mesh['dom_0'=8,'dom_1'=4,'group_0'=8,'group_1'=2] {'group_0','group_1'}, dimensions={0} | all-to-all | bytes 768 | tf_op jit(solution)/shard_map/all_to_all | solution.py:137
  19.0 2.8 %gather_fusion = bf16[96,16,256]{2,1,0:T(8,128)(2,1)} fusion(bf16[128,16,256]{2,1,0:T(8,128)(2,1)} %bitcast.72, s32[1024]{0:T(1024)S(1)} %pad_clamp_fusion.1), kind=kCustom, calls=%fused_computation | custom fusion | bytes 1573248 | tf_op jit(solution)/shard_map/gather | solution.py:142
  21.8 4.1 %all-to-all-start.1 = ((bf16[16,96,256]{2,1,0:T(8,128)(2,1)}), bf16[16,96,256]{2,1,0:T(8,128)(2,1)S(1)}, u32[]{:S(2)}, u32[]{:S(2)}) async-start(bf16[16,96,256]{2,1,0:T(8,128)(2,1)} %bitcast.6), calls=%async_computation.1 | async-start | bytes 1572864 | tf_op jit(solution)/shard_map/all_to_all | solution.py:143
  26.2 4.0 %convert_reduce_fusion = bf16[16,128,128]{2,1,0:T(8,128)(2,1)S(1)} fusion(s32[16,128,10]{1,2,0:T(8,128)S(1)} %copy.47), kind=kLoop, calls=%fused_computation.4 | loop fusion | flops 7602176 | bytes 606208 | tf_op jit(solution)/shard_map/reduce_sum | solution.py:86
  30.2 18.4 %all-to-all-done.1 = bf16[16,96,256]{2,1,0:T(8,128)(2,1)S(1)} async-done(((bf16[16,96,256]{2,1,0:T(8,128)(2,1)}), bf16[16,96,256]{2,1,0:T(8,128)(2,1)S(1)}, u32[]{:S(2)}, u32[]{:S(2)}) %all-to-all-start.1) | async-done | bytes 786464 | tf_op jit(solution)/shard_map/all_to_all | solution.py:143
  50.0 2.1 gather_fusion.1
  57.5 2.6 %copy.51 = f32[16,128,128]{2,1,0:T(8,128)} copy(f32[16,128,128]{1,2,0:T(8,128)} %get-tuple-element.11) | data formatting | bytes 2097152 | tf_op jit(solution)/shard_map/mul | solution.py:98
  60.1 3.9 %select_reduce_fusion.1 = f32[16,128,4]{1,2,0:T(4,128)S(1)} fusion(f32[16,128,128]{2,1,0:T(8,128)} %copy.51, s32[16,128,4]{1,2,0:T(4,128)S(1)} %bitcast.81), kind=kLoop, calls=%fused_computation.7 | loop fusion | flops 3137536 | bytes 1114112 | tf_op jit(solution)/shard_map/reduce_sum | solution.py:102
  64.7 3.8 %select_reduce_fusion = f32[16,128,128]{2,1,0:T(8,128)} fusion(f32[16,128,4]{1,2,0:T(4,128)S(1)} %get-tuple-element.4, s32[16,128,4]{1,2,0:T(4,128)S(1)} %bitcast.82), kind=kLoop, calls=%fused_computation.6 | loop fusion | flops 2883584 | bytes 1114112 | tf_op jit(solution)/shard_map/reduce_sum | solution.py:107
  68.4 2.6 %copy.53 = f32[16,128,128]{1,2,0:T(8,128)} copy(f32[16,128,128]{2,1,0:T(8,128)} %select_reduce_fusion) | data formatting | bytes 2097152 | tf_op jit(solution)/shard_map/reduce_sum | solution.py:107
  78.4 27.9 %all_to_all.48 = f32[64,8,257]{2,1,0:T(8,128)S(1)} all-to-all(f32[64,8,257]{2,1,0:T(8,128)S(1)} %copy.57), channel_id=1, replica_groups=mesh['dom_0'=8,'dom_1'=4,'group_0'=8,'group_1'=2] {'dom_1','group_0','gr..., dimensions={0} | all-to-all | bytes 1052672 | tf_op jit(solution)/shard_map/all_to_all | solution.py:27
  106.5 16.4 %all_to_all.49 = f32[8,1,257]{2,1,0:T(1,128)S(1)} all-to-all(f32[8,1,257]{2,1,0:T(1,128)S(1)} %all_to_all.35), channel_id=1, replica_groups=mesh['dom_0'=8,'dom_1'=4,'group_0'=8,'group_1'=2] {'dom_0'}, dimensions={0} | all-to-all | bytes 16448 | tf_op jit(solution)/shard_map/all_to_all | solution.py:34
  123.5 3.3 %all-to-all-start.5 = ((f32[8,1,257]{2,1,0:T(1,128)}), f32[8,1,257]{2,1,0:T(1,128)S(1)}, u32[]{:S(2)}, u32[]{:S(2)}) async-start(f32[8,1,257]{2,1,0:T(1,128)} %broadcast_in_dim.20), calls=%async_computation.5 | async-start | bytes 24576 | tf_op jit(solution)/shard_map/all_to_all | solution.py:46
  126.9 2.7 %fusion.24 = f32[2048,512]{1,0:T(8,128)} fusion(bf16[2048,256]{1,0:T(8,128)(2,1)S(1)} %fusion.5, bf16[512,256]{1,0:T(8,128)(2,1)S(1)} %copy-done), kind=kOutput, calls=%fused_computation.63 | convolution fusion | flops 536870912 | bytes 5505024 | tf_op jit(solution)/shard_map/dot_general | solution.py:118
  129.6 3.9 %all-to-all-done.5 = f32[8,1,257]{2,1,0:T(1,128)S(1)} async-done(((f32[8,1,257]{2,1,0:T(1,128)}), f32[8,1,257]{2,1,0:T(1,128)S(1)}, u32[]{:S(2)}, u32[]{:S(2)}) %all-to-all-start.5) | async-done | bytes 8256 | tf_op jit(solution)/shard_map/all_to_all | solution.py:46
  134.4 9.0 %all-to-all-start.6 = ((f32[64,8,257]{2,1,0:T(8,128)}), f32[64,8,257]{2,1,0:T(8,128)S(1)}, u32[]{:S(2)}, u32[]{:S(2)}) async-start(f32[64,8,257]{2,1,0:T(8,128)} %broadcast_in_dim.21), calls=%async_computation.6 | async-start | bytes 1572864 | tf_op jit(solution)/shard_map/all_to_all | solution.py:46
  148.5 2.3 broadcast_in_dim.16
  150.7 17.4 %scatter_fusion = f32[224,16,256]{2,1,0:T(8,128)} fusion(f32[224,16,256]{2,1,0:T(8,128)} %broadcast_in_dim.16, s32[128]{0:T(128)S(1)} %fusion.15, f32[128,16,256]{2,1,0:T(8,128)} %bitcast.66), kind=kCustom, calls=%fused_computation.2 | custom fusion | flops 524288 | bytes 6291968 | tf_op jit(solution)/shard_map/scatter-add | solution.py:156
  168.1 2.7 %slice.43 = f32[96,16,256]{2,1,0:T(8,128)} slice(f32[224,16,256]{2,1,0:T(8,128)} %scatter_fusion), slice={[128:224], [0:16], [0:256]} | slice | bytes 3145728 | tf_op jit(solution)/shard_map/slice | solution.py:158
  170.8 7.3 %all-to-all-start.2 = ((f32[16,96,256]{2,1,0:T(8,128)}), f32[16,96,256]{2,1,0:T(8,128)}, u32[]{:S(2)}, u32[]{:S(2)}) async-start(f32[16,96,256]{2,1,0:T(8,128)} %bitcast.68), calls=%async_computation.2 | async-start | bytes 3145728 | tf_op jit(solution)/shard_map/all_to_all | solution.py:159
  178.1 3.4 %slice_add_fusion = f32[128,16,256]{2,1,0:T(8,128)} fusion(f32[128,16,256]{2,1,0:T(8,128)S(1)} %bitcast.65, f32[224,16,256]{2,1,0:T(8,128)} %scatter_fusion), kind=kLoop, calls=%fused_computation.9 | loop fusion | flops 524288 | bytes 6291456 | tf_op jit(solution)/shard_map/add | solution.py:157
  187.7 1.9 slice_multiply_fusion.1
  189.6 27.2 %all-to-all-done.2 = f32[16,96,256]{2,1,0:T(8,128)} async-done(((f32[16,96,256]{2,1,0:T(8,128)}), f32[16,96,256]{2,1,0:T(8,128)}, u32[]{:S(2)}, u32[]{:S(2)}) %all-to-all-start.2) | async-done | bytes 1572896 | tf_op jit(solution)/shard_map/all_to_all | solution.py:159
  216.8 8.9 %scatter_fusion.1 = f32[128,16,256]{2,1,0:T(8,128)S(1)} fusion(f32[128,16,256]{2,1,0:T(8,128)S(1)} %copy-done.3, s32[96]{0:T(128)S(1)} %fusion.16, f32[96,16,256]{2,1,0:T(8,128)} %bitcast.17), kind=kCustom, calls=%fused_computation.3 | custom fusion | flops 393216 | bytes 4718976 | tf_op jit(solution)/shard_map/scatter-add | solution.py:166
  (82 shorter events, 29.8 us)
Async XLA Ops:
  0.6 52.0 %copy-start = (bf16[512,256]{1,0:T(8,128)(2,1)S(1)}, bf16[512,256]{1,0:T(8,128)(2,1)}, u32[]{:S(2)}) copy-start(bf16[512,256]{1,0:T(8,128)(2,1)} %param.13) | copy-start | bytes 786436
  0.6 25.2 %copy-start.17 = (s32[16,8]{0,1:T(8,128)S(1)}, s32[16,8]{0,1:T(8,128)}, u32[]{:S(2)}) copy-start(s32[16,8]{0,1:T(8,128)} %param.10) | copy-start | bytes 1540
  0.7 25.4 %copy-start.16 = (s32[2048,10]{0,1:T(8,128)S(1)}, s32[2048,10]{0,1:T(8,128)}, u32[]{:S(2)}) copy-start(s32[2048,10]{0,1:T(8,128)} %param.11) | copy-start | bytes 245764
  19.0 29.7 %copy-start.9 = (bf16[2048,256]{1,0:T(8,128)(2,1)S(1)}, bf16[2048,256]{1,0:T(8,128)(2,1)}, u32[]{:S(2)}) copy-start(bf16[2048,256]{1,0:T(8,128)(2,1)} %param.7) | copy-start | bytes 3145732
  21.8 26.8 %all-to-all-start.1 = ((bf16[16,96,256]{2,1,0:T(8,128)(2,1)}), bf16[16,96,256]{2,1,0:T(8,128)(2,1)S(1)}, u32[]{:S(2)}, u32[]{:S(2)}) async-start(bf16[16,96,256]{2,1,0:T(8,128)(2,1)} %bitcast.6), calls=%async_computation.1 | async-start | bytes 1572864 | tf_op jit(solution)/shard_map/all_to_all | solution.py:143
  30.2 22.0 %copy-start.5 = (bf16[16,128,128]{2,1,0:T(8,128)(2,1)}, bf16[16,128,128]{2,1,0:T(8,128)(2,1)S(1)}, u32[]{:S(2)}) copy-start(bf16[16,128,128]{2,1,0:T(8,128)(2,1)S(1)} %convert_reduce_fusion) | copy-start | bytes 1572868
  52.2 1.2 copy-start.10
  52.6 1.9 copy-start.13
  55.1 1.0 copy-start.7
  56.1 4.0 %copy-start.15 = (s32[2048,4]{0,1:T(4,128)S(1)}, s32[2048,4]{0,1:T(4,128)}, u32[]{:S(2)}) copy-start(s32[2048,4]{0,1:T(4,128)} %param.12) | copy-start | bytes 98308
  73.7 1.5 copy-start.11
  73.7 1.5 copy-start.14
  123.5 9.9 %all-to-all-start.5 = ((f32[8,1,257]{2,1,0:T(1,128)}), f32[8,1,257]{2,1,0:T(1,128)S(1)}, u32[]{:S(2)}, u32[]{:S(2)}) async-start(f32[8,1,257]{2,1,0:T(1,128)} %broadcast_in_dim.20), calls=%async_computation.5 | async-start | bytes 24576 | tf_op jit(solution)/shard_map/all_to_all | solution.py:46
  129.6 13.8 %copy-start.2 = (f32[16,128,128]{1,2,0:T(8,128)S(1)}, f32[16,128,128]{1,2,0:T(8,128)}, u32[]{:S(2)}) copy-start(f32[16,128,128]{1,2,0:T(8,128)} %copy.53) | copy-start | bytes 3145732
  129.6 13.9 %copy-start.8 = (bf16[2048,256]{1,0:T(8,128)(2,1)S(1)}, bf16[2048,256]{1,0:T(8,128)(2,1)}, u32[]{:S(2)}) copy-start(bf16[2048,256]{1,0:T(8,128)(2,1)} %copy-done.7) | copy-start | bytes 3145732
  134.4 36.4 %all-to-all-start.6 = ((f32[64,8,257]{2,1,0:T(8,128)}), f32[64,8,257]{2,1,0:T(8,128)S(1)}, u32[]{:S(2)}, u32[]{:S(2)}) async-start(f32[64,8,257]{2,1,0:T(8,128)} %broadcast_in_dim.21), calls=%async_computation.6 | async-start | bytes 1572864 | tf_op jit(solution)/shard_map/all_to_all | solution.py:46
  143.4 2.2 copy-start.1
  145.6 1.0 copy-start.6
  170.8 10.7 %copy-start.12 = (f32[64,8,257]{2,1,0:T(8,128)}, f32[64,8,257]{2,1,0:T(8,128)S(1)}, u32[]{:S(2)}) copy-start(f32[64,8,257]{2,1,0:T(8,128)S(1)} %all-to-all-done.6) | copy-start | bytes 1579012
  170.8 45.9 %all-to-all-start.2 = ((f32[16,96,256]{2,1,0:T(8,128)}), f32[16,96,256]{2,1,0:T(8,128)}, u32[]{:S(2)}, u32[]{:S(2)}) async-start(f32[16,96,256]{2,1,0:T(8,128)} %bitcast.68), calls=%async_computation.2 | async-start | bytes 3145728 | tf_op jit(solution)/shard_map/all_to_all | solution.py:159
  182.8 34.0 %copy-start.3 = (f32[128,16,256]{2,1,0:T(8,128)S(1)}, f32[128,16,256]{2,1,0:T(8,128)}, u32[]{:S(2)}) copy-start(f32[128,16,256]{2,1,0:T(8,128)} %slice_add_fusion) | copy-start | bytes 6291460
  225.7 1.3 copy-start.4
where the time goes:
time: 230 us; the launch traced here: 228 us
  blocking collectives  60.7 us (26%)
  other arithmetic  49.7 us (22%)
  waiting for transfers between devices  49.5 us (22%)
  local copies, waits for them, and re-layouts  30.8 us (13%)
  starting transfers between devices  23.7 us (10%)
  matrix products  10.3 us (4%)
  between operations  3.47 us (2%)
    all_to_all x1, blocking collectives, sent_and_summed(): lax.all_to_all(cut_along(array, dim, length), axis, 0, 0, tiled=True)  27.9 us
    all_to_all x1, waiting for transfers between devices, per_device(): lax.all_to_all(incoming.reshape(peer_count, capacity * BLK, feature_width...  27.2 us
    all_to_all x1, waiting for transfers between devices, per_device(): lax.all_to_all(outgoing, GROUP, split_axis=0, concat_axis=0, tiled=True)  18.4 us
    scatter-add x1, other arithmetic, per_device(): table_grad.at[slot_list].add(dcandidates.reshape(-1, BLK, feature_width))  17.4 us
    all_to_all x1, blocking collectives, sum_by_axis(): return jnp.sum(lax.all_to_all(own, far, 0, 0, tiled=True), axis=0)  16.4 us
    all_to_all x1, blocking collectives, per_device(): lax.all_to_all(request, GROUP, split_axis=0, concat_axis=0, tiled=True)  16.3 us
    all_to_all x2, starting transfers between devices, from_everyone(): return lax.all_to_all(copies, axis, split_axis=0, concat_axis=0, tiled=True)  12.3 us
    scatter-add x1, other arithmetic, per_device(): own_grad.at[picked.reshape(-1)]  8.94 us
  transfers between devices with their start and end apart: 4, of which 3 were waited for; matrix products, arithmetic and copies ran while one was open for 19% of the time, Pallas kernels for 0%

commit v1 on v0

v1 whole, which is shorter than its diff:
```python
import functools

import jax
import jax.numpy as jnp
from jax import lax
from jax.experimental import pallas as pl
from jax.experimental.pallas import tpu as pltpu
from jax.sharding import Mesh
from jax.sharding import PartitionSpec as P

MESH = pl.DeviceIdType.MESH
TILE = 128
BLK = 16
NBT = 8
DEG = 10
NNEG = 4
CAP = 6
TILES = 16
NODES = 2048
D = 256
NBD = 128
NBND = 16
ROWS = NBND * BLK
PEERS = 16
TABLE = NODES + PEERS * ROWS
NY = 8
NZ = 8
NX = 4
f32 = jnp.float32
bf16 = jnp.bfloat16
AXES = ("z", "x", "y", "c")


def place():
    return tuple(lax.axis_index(a) for a in AXES)


def remote(src, dst, send, recv, device):
    return pltpu.make_async_remote_copy(
        src_ref=src, dst_ref=dst, send_sem=send, recv_sem=recv, device_id=device, device_id_type=MESH
    )


SUBS = 4
SUB = ROWS // SUBS


def gather_kernel(boundary, feat, out, buf, rs, rr, ls, lr, cs, cr, outs):
    z, x, y, c = place()
    right = (z, x, lax.rem(y + 1, NY), c)
    left = (z, x, lax.rem(y + NY - 1, NY), c)
    mate = (z, x, y, 1 - c)

    def slot(yy, cc):
        return lax.rem(yy + NY, NY) * 2 + cc

    me = slot(y, c)
    for p in range(NBND):
        buf[me, pl.ds(p * BLK, BLK), :] = feat[boundary[p]]
    barrier = pltpu.get_barrier_semaphore()
    for d in (right, left, mate):
        pl.semaphore_signal(barrier, inc=1, device_id=d, device_id_type=MESH)
    pl.semaphore_wait(barrier, 3)

    def piece(s, q):
        return buf.at[s, pl.ds(q * SUB, SUB), :]

    def to_right(d, q):
        v = piece(slot(y - d, c), q)
        return remote(v, v, rs.at[d, q], rr.at[d, q], right)

    def from_left(d, q):
        v = piece(slot(y - 1 - d, c), q)
        return remote(v, v, rs.at[d, q], rr.at[d, q], right)

    def to_left(d, q):
        v = piece(slot(y + d, c), q)
        return remote(v, v, ls.at[d, q], lr.at[d, q], left)

    def from_right(d, q):
        v = piece(slot(y + 1 + d, c), q)
        return remote(v, v, ls.at[d, q], lr.at[d, q], left)

    def to_mate(k, s, q):
        v = piece(s, q)
        return remote(v, v, cs.at[k, q], cr.at[k, q], mate)

    def from_mate(k, s, q):
        v = piece(s, q)
        return remote(v, v, cs.at[k, q], cr.at[k, q], mate)

    half = SUBS // 2
    sent = []

    def go(copy):
        copy.start()
        sent.append(copy)

    for q in range(SUBS):
        go(to_right(0, q))
        go(to_left(0, SUBS - 1 - q))
    for q in range(SUBS):
        go(to_mate(0, me, q))
    for d in range(1, 5):
        for q in range(SUBS):
            if d < 4 or q < half:
                from_left(d - 1, q).wait_recv()
                if d < 3 or (d == 3 and q < half):
                    go(to_right(d, q))
                go(to_mate(d, slot(y - d, c), q))
            b = SUBS - 1 - q
            if d < 4 or b >= half:
                from_right(d - 1, b).wait_recv()
                if d < 3 or (d == 3 and b >= half):
                    go(to_left(d, b))
                go(to_mate(d if d == 4 else 8 - d, slot(y + d, c), b))
    o = 1 - c
    for k in range(8):
        for q in range(SUBS):
            from_mate(k, slot(y - k, o), q).wait_recv()
    copy = pltpu.make_async_copy(buf, out, outs)
    copy.start()
    for s in sent:
        s.wait_send()
    copy.wait()


def gathered(boundary, features):
    sem = pltpu.SemaphoreType.DMA
    return pl.pallas_call(
        gather_kernel,
        out_shape=jax.ShapeDtypeStruct((PEERS, ROWS, D), bf16),
        in_specs=[pl.BlockSpec(memory_space=pltpu.SMEM), pl.BlockSpec(memory_space=pltpu.VMEM)],
        out_specs=pl.BlockSpec(memory_space=pl.ANY),
        scratch_shapes=[
            pltpu.VMEM((PEERS, ROWS, D), bf16),
            sem((4, SUBS)),
            sem((4, SUBS)),
            sem((4, SUBS)),
            sem((4, SUBS)),
            sem((8, SUBS)),
            sem((8, SUBS)),
            sem(()),
        ],
        compiler_params=pltpu.CompilerParams(collective_id=0, has_side_effects=True),
        name="boundary_gather",
    )(boundary, features)


def over(a, b, da, db):
    return lax.dot_general(a, b, (((da,), (db,)), ((), ())), preferred_element_type=f32)


def layer_kernel(
    slots, req, nbr, neg, weight, feat_hbm, far_hbm,
    own_out, far_out, dw_out, loss_out,
    table, grads, aggs, dpres, sems,
):
    c1 = pltpu.make_async_copy(feat_hbm, table.at[pl.ds(0, NODES), :], sems.at[0])
    c2 = pltpu.make_async_copy(far_hbm, table.at[pl.ds(NODES, PEERS * ROWS), :], sems.at[1])
    c1.start()
    c2.start()

    @pl.loop(0, TABLE // 256)
    def _(i):
        grads[pl.ds(pl.multiple_of(i * 256, 256), 256), :] = jnp.zeros((256, D), f32)

    c1.wait()
    c2.wait()
    kio = lax.broadcasted_iota(jnp.int32, (TILE, TILE), 0)
    inv_root = D ** (-0.5)

    def tile(t, loss):
        base = pl.multiple_of(t * TILE, TILE)
        rows = []
        for j in range(NBT):
            s = slots[j, t]
            n = jnp.maximum(s - NBD, 0)
            e = (n * 43) >> 8
            b = jnp.where(s < NBD, s, NBD + e * NBND + req[n - e * CAP, e])
            rows.append(pl.multiple_of(b * BLK, BLK))
        cand = jnp.concatenate([table[pl.ds(r, BLK), :] for r in rows], axis=0)
        nb = nbr[:, pl.ds(base, TILE)]
        ng = neg[:, pl.ds(base, TILE)]
        counts = jnp.zeros((TILE, TILE), f32)
        for j in range(DEG):
            counts += jnp.where(nb[j : j + 1, :] == kio, 1.0, 0.0)
        counts = counts.astype(bf16)
        x = table[pl.ds(base, TILE), :]
        agg = (over(counts, cand, 0, 0) / DEG).astype(bf16)
        pre = over(x, weight[:D, :], 1, 0) + over(agg, weight[D:, :], 1, 0)
        gate = jax.nn.sigmoid(pre)
        hid = pre * gate
        scale = lax.rsqrt(jnp.mean(hid * hid, axis=-1, keepdims=True) + 1e-06)
        emb = hid * scale
        eh = emb.astype(bf16)
        sc = over(cand, eh, 1, 1) * inv_root
        pos = nb[0:1, :] == kio
        ps = jnp.sum(jnp.where(pos, sc, 0.0), axis=0, keepdims=True)
        negs = [ng[n : n + 1, :] == kio for n in range(NNEG)]
        ns = [jnp.sum(jnp.where(m, sc, 0.0), axis=0, keepdims=True) for m in negs]
        ex = 0.5 + jnp.concatenate(ns, axis=0) - ps
        loss += jax.nn.softplus(ex) * 0.25
        w = jax.nn.sigmoid(ex) * 0.25
        wsum = jnp.sum(w, axis=0, keepdims=True)
        ds = jnp.where(negs[0], w[0:1, :], 0.0)
        for n in range(1, NNEG):
            ds += jnp.where(negs[n], w[n : n + 1, :], 0.0)
        ds = (ds - jnp.where(pos, wsum, 0.0)) * inv_root
        ds = ds.astype(bf16)
        demb = over(ds, cand, 0, 0)
        m2 = jnp.mean(demb * emb, axis=-1, keepdims=True)
        dh = scale * (demb - emb * m2)
        dpre = (dh * gate * (1.0 + pre * (1.0 - gate))).astype(bf16)
        aggs[pl.ds(base, TILE), :] = agg
        dpres[pl.ds(base, TILE), :] = dpre
        dself = over(dpre, weight[:D, :], 1, 1)
        dagg = (over(dpre, weight[D:, :], 1, 1) / DEG).astype(bf16)
        dc = over(ds, eh, 1, 0) + over(counts, dagg, 1, 0)
        grads[pl.ds(base, TILE), :] += dself
        for j in range(NBT):
            grads[pl.ds(rows[j], BLK), :] += dc[j * BLK : (j + 1) * BLK, :]
        return loss

    loss = lax.fori_loop(0, TILES, tile, jnp.zeros((NNEG, TILE), f32))
    o1 = pltpu.make_async_copy(grads.at[pl.ds(NODES, PEERS * ROWS), :], far_out, sems.at[2])
    o2 = pltpu.make_async_copy(grads.at[pl.ds(0, NODES), :], own_out, sems.at[3])
    o1.start()
    o2.start()
    dp = dpres[...]
    for h in range(2):
        src = table[pl.ds(0, NODES), :] if h == 0 else aggs[...]
        dw = over(src, dp, 0, 0)
        for l in range(2):
            dw_out[l * 512 + h * 256 : l * 512 + h * 256 + 256, :] = dw[:, l * 128 : l * 128 + 128]
    loss_out[...] = jnp.broadcast_to(jnp.sum(loss, keepdims=True), (8, 128))
    o1.wait()
    o2.wait()


def layer(slots, req, nbr, neg, weight, features, far):
    vm = pl.BlockSpec(memory_space=pltpu.VMEM)
    sm = pl.BlockSpec(memory_space=pltpu.SMEM)
    hbm = pl.BlockSpec(memory_space=pl.ANY)
    return pl.pallas_call(
        layer_kernel,
        out_shape=(
            jax.ShapeDtypeStruct((NODES, D), f32),
            jax.ShapeDtypeStruct((PEERS * ROWS, D), f32),
            jax.ShapeDtypeStruct((1024, 128), f32),
            jax.ShapeDtypeStruct((8, 128), f32),
        ),
        in_specs=[sm, sm, vm, vm, vm, hbm, hbm],
        out_specs=(hbm, hbm, vm, vm),
        scratch_shapes=[
            pltpu.VMEM((TABLE, D), bf16),
            pltpu.VMEM((TABLE, D), f32),
            pltpu.VMEM((NODES, D), bf16),
            pltpu.VMEM((NODES, D), bf16),
            pltpu.SemaphoreType.DMA((4,)),
        ],
        name="layer",
    )(slots, req, nbr, neg, weight, features, far)


HALF = ROWS // 2


def reduce_kernel(
    part, dw, lossp, out, dw_out, loss_out,
    mine, mates, rbuf, lbuf, rsend, lsend,
    w0, sum0, lossb, a1, b1, a2, b2, sum1, sum3, sum2, ybuf, total, ag2a, ag2b, ag1,
    ms, mr, lsem, rs, rr, ls, lr, ws, wr,
):
    z, x, y, c = place()
    o = 1 - c
    right = (z, x, lax.rem(y + 1, NY), c)
    left = (z, x, lax.rem(y + NY - 1, NY), c)
    mate = (z, x, y, o)

    def zs(k):
        return (lax.rem(z + k, NZ), x, y, c)

    def xs(k):
        return (z, lax.rem(x + k, NX), y, c)

    def ys(k):
        return (z, x, lax.rem(y + k, NY), c)

    peers = [mate] + [zs(k) for k in range(1, NZ)] + [xs(k) for k in range(1, NX)] + [ys(k) for k in range(1, NY)]
    barrier = pltpu.get_barrier_semaphore()
    for d in peers:
        pl.semaphore_signal(barrier, inc=1, device_id=d, device_id_type=MESH)
    pl.semaphore_wait(barrier, len(peers))

    sent = []

    def go(copy):
        copy.start()
        sent.append(copy)
        return copy

    def rows(first, n):
        return pl.ds(pl.multiple_of(first, 8), n)

    first = [
        remote(dw.at[rows(o * 512, 512), :], w0, ws.at[0, 0], wr.at[0, 0], mate),
        remote(lossp, lossb.at[0], ws.at[0, 1], wr.at[0, 1], mate),
    ]
    for copy in first:
        go(copy)

    def owner(k):
        return lax.rem(y + k + NY, NY)

    order = [4, 3, -3, 2, -2, 1, -1, 0]
    mcopies = {}
    for i, k in enumerate(order):
        oo = owner(k)
        lc = pltpu.make_async_copy(part.at[rows((oo * 2 + c) * ROWS, ROWS), :], mine.at[i], lsem.at[i])
        lc.start()
        rc = go(remote(part.at[rows((oo * 2 + o) * ROWS, ROWS), :], mates.at[i], ms.at[i], mr.at[i], mate))
        mcopies[k] = (lc, rc)
    ready = {}

    def pair(k, h):
        if k not in ready:
            lc, rc = mcopies[k]
            lc.wait()
            rc.wait_recv()
            ready[k] = True
        i = order.index(k)
        return mine[i, h * HALF : (h + 1) * HALF, :] + mates[i, h * HALF : (h + 1) * HALF, :]

    def hop(to_right, s, h):
        sb, rb, ss, rsm, dev = (rsend, rbuf, rs, rr, right) if to_right else (lsend, lbuf, ls, lr, left)
        view = pl.ds(h * HALF, HALF)
        return remote(sb.at[s, view, :], rb.at[s, view, :], ss.at[s, h], rsm.at[s, h], dev)

    def ring(to_right, s, h):
        start = 0 if (h == 0) == to_right else 1
        if s < start:
            return
        k = 4 - s if to_right else (-(4 - s) if s else 4)
        v = pair(k, h)
        if s > start:
            hop(to_right, s - 1, h).wait_recv()
            v = v + (rbuf if to_right else lbuf)[s - 1, h * HALF : (h + 1) * HALF, :]
        (rsend if to_right else lsend)[s, h * HALF : (h + 1) * HALF, :] = v
        go(hop(to_right, s, h))

    def r0():
        ring(True, 0, 0)
        ring(False, 0, 1)

    def r1a():
        ring(True, 1, 1)
        ring(False, 1, 0)

    def r1b():
        ring(True, 1, 0)
        ring(False, 1, 1)

    def r2a():
        ring(True, 2, 1)
        ring(False, 2, 0)

    def r2b():
        ring(True, 2, 0)
        ring(False, 2, 1)

    def r3a():
        ring(True, 3, 1)
        ring(False, 3, 0)

    def r3b():
        ring(True, 3, 0)
        ring(False, 3, 1)

    def r4():
        for h in (1, 0):
            v = pair(0, h)
            hop(True, 3, h).wait_recv()
            hop(False, 3, h).wait_recv()
            view = slice(h * HALF, (h + 1) * HALF)
            out[view, :] = v + rbuf[3, view, :] + lbuf[3, view, :]

    def scatter(stage, src, base, r, buf, n, me, dev):
        buf[me] = src[rows(base + me * r, r), :]
        for k in range(1, n):
            to = lax.rem(me + k, n)
            go(remote(src.at[rows(base + to * r, r), :], buf.at[me], ws.at[stage, k], wr.at[stage, me], dev(k)))

    def arrived(stage, buf, n, me, dev):
        for k in range(1, n):
            who = lax.rem(me + k, n)
            remote(buf.at[who], buf.at[who], ws.at[stage, k], wr.at[stage, who], dev(k)).wait_recv()

    def spread(stage, src, buf, n, me, dev):
        buf[me] = src[...]
        for k in range(1, n):
            go(remote(src, buf.at[me], ws.at[stage, k], wr.at[stage, me], dev(k)))

    def summed(buf, n):
        v = buf[0]
        for i in range(1, n):
            v = v + buf[i]
        return v

    lz, lx, lossz, lossx = lossb.at[pl.ds(2, NZ)], lossb.at[pl.ds(10, NX)], lossb.at[14], lossb.at[15]

    def wa():
        for copy in first:
            copy.wait_recv()
        sum0[...] = dw[rows(c * 512, 512), :] + w0[...]
        lossb[1] = lossp[...] + lossb[0]
        scatter(1, sum0, 0, 32, a1, NZ, z, zs)
        scatter(2, sum0, 256, 64, b1, NX, x, xs)
        spread(3, lossb.at[1], lz, NZ, z, zs)

    def wb():
        arrived(2, b1, NX, x, xs)
        sum1[32:96, :] = summed(b1, NX)
        scatter(4, sum1, 32, 8, b2, NZ, z, zs)

    def wc():
        arrived(1, a1, NZ, z, zs)
        arrived(3, lz, NZ, z, zs)
        sum1[0:32, :] = summed(a1, NZ)
        lossb[14] = summed(lz, NZ)
        scatter(5, sum1, 0, 8, a2, NX, x, xs)
        spread(6, lossz, lx, NX, x, xs)

    def wd():
        arrived(4, b2, NZ, z, zs)
        arrived(5, a2, NX, x, xs)
        arrived(6, lx, NX, x, xs)
        sum2[0:8, :] = summed(a2, NX)
        sum2[8:16, :] = summed(b2, NZ)
        sum2[16:24, :] = summed(lx, NX)
        spread(7, sum2, ybuf, NY, y, ys)

    def we():
        arrived(7, ybuf, NY, y, ys)
        t = summed(ybuf, NY)
        total[...] = t
        loss_out[...] = t[16:24, :]
        spread(8, total.at[pl.ds(0, 8), :], ag2a, NX, x, xs)
        spread(9, total.at[pl.ds(8, 8), :], ag2b, NZ, z, zs)

    def wide(stage, src, r, base, n, me, dev):
        for k in range(1, n):
            go(remote(src, ag1.at[rows(base + me * r, r), :], ws.at[stage, k], wr.at[stage, me], dev(k)))

    def wide_arrived(stage, r, base, n, me, dev):
        for k in range(1, n):
            who = lax.rem(me + k, n)
            v = ag1.at[rows(base + who * r, r), :]
            remote(v, v, ws.at[stage, k], wr.at[stage, who], dev(k)).wait_recv()

    def wf():
        arrived(8, ag2a, NX, x, xs)
        for i in range(NX):
            sum3[i * 8 : i * 8 + 8, :] = ag2a[i]
        wide(10, sum3.at[pl.ds(0, 32), :], 32, 0, NZ, z, zs)
        ag1[rows(z * 32, 32), :] = sum3[0:32, :]

    def wg():
        arrived(9, ag2b, NZ, z, zs)
        for i in range(NZ):
            sum3[32 + i * 8 : 40 + i * 8, :] = ag2b[i]
        wide(11, sum3.at[pl.ds(32, 64), :], 64, 256, NX, x, xs)
        ag1[rows(256 + x * 64, 64), :] = sum3[32:96, :]

    last = []

    def wh():
        wide_arrived(11, 64, 256, NX, x, xs)
        last.append(go(remote(ag1.at[pl.ds(256, 256), :], dw_out.at[rows(c * 512 + 256, 256), :], ws.at[12, 1], wr.at[12, 1], mate)))
        dw_out[rows(c * 512 + 256, 256), :] = ag1[256:512, :]

    def wi():
        wide_arrived(10, 32, 0, NZ, z, zs)
        last.append(go(remote(ag1.at[pl.ds(0, 256), :], dw_out.at[rows(c * 512, 256), :], ws.at[12, 0], wr.at[12, 0], mate)))
        dw_out[rows(c * 512, 256), :] = ag1[0:256, :]
        for copy in last:
            copy.wait_recv()

    for step in (wa, r0, r1a, wb, r1b, r2a, wc, wd, r2b, we, r3a, wg, wf, r3b, wh, r4, wi):
        step()
    for copy in sent:
        copy.wait_send()


def reduced(part, dw, lossp):
    vm = pl.BlockSpec(memory_space=pltpu.VMEM)
    hbm = pl.BlockSpec(memory_space=pl.ANY)
    sem = pltpu.SemaphoreType.DMA
    V = pltpu.VMEM
    return pl.pallas_call(
        reduce_kernel,
        out_shape=(
            jax.ShapeDtypeStruct((ROWS, D), f32),
            jax.ShapeDtypeStruct((1024, 128), f32),
            jax.ShapeDtypeStruct((8, 128), f32),
        ),
        in_specs=[hbm, vm, vm],
        out_specs=(vm, vm, vm),
        scratch_shapes=[
            V((8, ROWS, D), f32),
            V((8, ROWS, D), f32),
            V((4, ROWS, D), f32),
            V((4, ROWS, D), f32),
            V((4, ROWS, D), f32),
            V((4, ROWS, D), f32),
            V((512, 128), f32),
            V((512, 128), f32),
            V((16, 8, 128), f32),
            V((NZ, 32, 128), f32),
            V((NX, 64, 128), f32),
            V((NX, 8, 128), f32),
            V((NZ, 8, 128), f32),
            V((96, 128), f32),
            V((96, 128), f32),
            V((24, 128), f32),
            V((NY, 24, 128), f32),
            V((24, 128), f32),
            V((NX, 8, 128), f32),
            V((NZ, 8, 128), f32),
            V((512, 128), f32),
            sem((8,)),
            sem((8,)),
            sem((8,)),
            sem((4, 2)),
            sem((4, 2)),
            sem((4, 2)),
            sem((4, 2)),
            sem((13, 8)),
            sem((13, 8)),
        ],
        compiler_params=pltpu.CompilerParams(collective_id=1, has_side_effects=True),
        name="sums",
    )(part, dw, lossp)


def add_kernel(boundary, got, own, out, buf, rsem, wsem):
    for p in range(NBND):
        row = pl.multiple_of(boundary[p] * BLK, BLK)
        pltpu.make_async_copy(own.at[pl.ds(row, BLK), :], buf.at[pl.ds(p * BLK, BLK), :], rsem.at[p]).start()
    for p in range(NBND):
        row = pl.multiple_of(boundary[p] * BLK, BLK)
        view = pl.ds(p * BLK, BLK)
        pltpu.make_async_copy(own.at[pl.ds(row, BLK), :], buf.at[view, :], rsem.at[p]).wait()
        buf[view, :] += got[view, :]
        pltpu.make_async_copy(buf.at[view, :], out.at[pl.ds(row, BLK), :], wsem.at[p]).start()
    for p in range(NBND):
        row = pl.multiple_of(boundary[p] * BLK, BLK)
        pltpu.make_async_copy(buf.at[pl.ds(p * BLK, BLK), :], out.at[pl.ds(row, BLK), :], wsem.at[p]).wait()


def added(boundary, got, own):
    hbm = pl.BlockSpec(memory_space=pl.ANY)
    return pl.pallas_call(
        add_kernel,
        out_shape=jax.ShapeDtypeStruct((NODES, D), f32),
        in_specs=[pl.BlockSpec(memory_space=pltpu.SMEM), pl.BlockSpec(memory_space=pltpu.VMEM), hbm],
        out_specs=hbm,
        scratch_shapes=[
            pltpu.VMEM((ROWS, D), f32),
            pltpu.SemaphoreType.DMA((NBND,)),
            pltpu.SemaphoreType.DMA((NBND,)),
        ],
        input_output_aliases={2: 0},
        name="add_returned",
    )(boundary, got, own)


def per_device(features, boundary, request, tile_slots, neighbors, negatives, layer_weight):
    far = gathered(boundary, features.reshape(NBD, BLK, D))
    own, part, dw, lossp = layer(
        tile_slots.T, request.T, neighbors.T, negatives.T, layer_weight, features, far.reshape(PEERS * ROWS, D)
    )
    got, dwt, losst = reduced(part, dw, lossp)
    grad = added(boundary, got, own)
    wgrad = jnp.concatenate([dwt[:512], dwt[512:]], axis=1) / NODES
    return grad, wgrad, losst[0, 0] / (NODES * 512)


def solution(mesh):
    finer = Mesh(mesh.devices.reshape(NZ, NX, NY, 2), AXES)
    dg = AXES
    return jax.shard_map(
        per_device,
        mesh=finer,
        in_specs=(P(dg, None), P(dg), P(dg, None), P(dg, None), P(dg, None), P(dg, None), P()),
        out_specs=(P(dg, None), P(), P()),
        check_vma=False,
    )
```

time: 230 us -> 107 us (0.47)
  Pallas kernels: 0 us -> 103 us
  blocking collectives: 60.7 us -> 0 us
  waiting for transfers between devices: 49.5 us -> 0 us
  other arithmetic: 49.7 us -> 0.83 us
  local copies, waits for them, and re-layouts: 30.8 us -> 1.23 us
  starting transfers between devices: 23.7 us -> 0 us
  matrix products: 10.3 us -> 0 us
    pallas_call x0 -> x4, Pallas kernels: none -> 103 us  [the longest x1 46.1 us: reduced(): pl.pallas_call(reduce_kernel, out_shape=(jax.ShapeDtypeStruct((ROWS, D),...]
    all_to_all x3 -> x0, blocking collectives: 60.7 us -> none  [the longest x1 27.9 us: sent_and_summed(): lax.all_to_all(cut_along(array, dim, length), axis, 0, 0, tiled=True)]
    all_to_all x4 -> x0, waiting for transfers between devices: 49.5 us -> none  [the longest x1 27.2 us: per_device(): lax.all_to_all(incoming.reshape(peer_count, capacity * BLK, feature_width...]
    scatter-add x2 -> x0, other arithmetic: 26.4 us -> none  [the longest x1 17.4 us: per_device(): table_grad.at[slot_list].add(dcandidates.reshape(-1, BLK, feature_width))]
    all_to_all x4 -> x0, starting transfers between devices: 23.7 us -> none  [the longest x2 12.3 us: from_everyone(): return lax.all_to_all(copies, axis, split_axis=0, concat_axis=0, tiled=True)]
    reduce_sum x8 -> x0, other arithmetic: 14.3 us -> none  [the longest x1 4.02 us: tile_terms(): jnp.sum((neighbor_ids[..., None] == slot_ids).astype(jnp.float32), axis=2)]
    dot_general x8 -> x0, matrix products: 10.3 us -> none  [the longest x5 5.78 us: contract(): return jnp.einsum(form, left, right, preferred_element_type=jnp.float32)]
    unnamed x40 -> x2, local copies, waits for them, and re-layouts: 5.99 us -> 0.01 us
  transfers between devices with their start and end apart: 4 -> 0, of which waited for: 3 -> 0; matrix products, arithmetic and copies ran while one was open for 19% -> 0% of each run, Pallas kernels for 0% -> 0%
where the time goes in v1:
time: 107 us
  Pallas kernels  103 us (96%)
  between operations  2.47 us (2%)
  local copies, waits for them, and re-layouts  1.23 us (1%)
    pallas_call x1, Pallas kernels, reduced(): pl.pallas_call(reduce_kernel, out_shape=(jax.ShapeDtypeStruct((ROWS, D),...  46.1 us
    pallas_call x1, Pallas kernels, layer(): pl.pallas_call(layer_kernel, out_shape=(jax.ShapeDtypeStruct((NODES, D),...  27.3 us
    pallas_call x1, Pallas kernels, gathered(): pl.pallas_call(gather_kernel, out_shape=jax.ShapeDtypeStruct((PEERS, ROWS...  26.3 us
    pallas_call x1, Pallas kernels, added(): pl.pallas_call(add_kernel, out_shape=jax.ShapeDtypeStruct((NODES, D), f32...  2.82 us

profile of v1, /device:TPU:1, one launch (start us, length us, event | category | flops | bytes accessed | tf_op | source)
XLA Modules:
  0.0 107.1 jit_solution(9649562925865182227)
XLA Ops:
  0.6 26.3 %boundary_gather.1 = bf16[16,256,256]{2,1,0:T(8,128)(2,1)} custom-call(s32[16]{0:T(128)} %boundary.3, bf16[128,16,256]{2,1,0:T(8,128)(2,1)} %bitcast.8), custom_call_target="tpu_custom_call" | custom-call | tf_op jit(solution)/shard_map/boundary_gather/pallas_call | solution.py:130
  27.0 27.3 %layer.1 = (f32[2048,256]{1,0:T(8,128)}, f32[4096,256]{1,0:T(8,128)}, f32[1024,128]{1,0:T(8,128)}, f32[8,128]{1,0:T(8,128)}) custom-call(s32[8,16]{1,0:T(8,128)} %bitcast.11, s32[6,16]{1,0:T(8,128)} %bitcast.12, s32[10,2048]{1,0:T(8,128)} %bitcast.9, s32[4,2048]{1,0:T(4,128)} %bitcast.10, bf16[512,256]{1,0:T(8,128)(2,1)} %weight.1, ...), custom_call_target="tpu_custom_call" | custom-call | tf_op jit(solution)/shard_map/layer/pallas_call | solution.py:245
  54.3 46.1 %sums.1 = (f32[256,256]{1,0:T(8,128)}, f32[1024,128]{1,0:T(8,128)}, f32[8,128]{1,0:T(8,128)}) custom-call(f32[4096,256]{1,0:T(8,128)} %get-tuple-element.10.part, f32[1024,128]{1,0:T(8,128)} %get-tuple-element.11.dw, f32[8,128]{1,0:T(8,128)} %get-tuple-element.12.lossp), custom_call_target="tpu_custom_call" | custom-call | tf_op jit(solution)/shard_map/sums/pallas_call | solution.py:500
  100.4 1.2 %slice.11 = f32[1,1]{1,0:T(1,128)} slice(f32[8,128]{1,0:T(8,128)} %get-tuple-element.16), slice={[0:1], [0:1]} | slice | bytes 8 | tf_op jit(solution)/shard_map/slice | solution.py:586
  102.2 0.0 copy-start
  102.2 2.8 %add_returned.1 = f32[2048,256]{1,0:T(8,128)} custom-call(s32[16]{0:T(128)} %boundary.3, f32[256,256]{1,0:T(8,128)} %get-tuple-element.13.got, f32[2048,256]{1,0:T(8,128)} %get-tuple-element.14.own), custom_call_target="tpu_custom_call", output_to_operand_aliasing={{}: (2, {})} | custom-call | tf_op jit(solution)/shard_map/add_returned/pallas_call | solution.py:563
  105.0 0.0 copy-done
  105.1 0.8 maximum_multiply_fusion
  (1 shorter events, 0.0 us)
Async XLA Ops:
  102.2 2.8 %copy-start = (f32[1024,128]{1,0:T(8,128)S(1)}, f32[1024,128]{1,0:T(8,128)}, u32[]{:S(2)}) copy-start(f32[1024,128]{1,0:T(8,128)} %get-tuple-element.15) | copy-start | bytes 1572868

commit v2 on v1

v2 whole, which is shorter than its diff:
```python
import functools

import jax
import jax.numpy as jnp
from jax import lax
from jax.experimental import pallas as pl
from jax.experimental.pallas import tpu as pltpu
from jax.sharding import Mesh
from jax.sharding import PartitionSpec as P

MESH = pl.DeviceIdType.MESH
TILE = 128
BLK = 16
NBT = 8
DEG = 10
NNEG = 4
CAP = 6
TILES = 16
NODES = 2048
D = 256
NBD = 128
NBND = 16
ROWS = NBND * BLK
PEERS = 16
TABLE = NODES + PEERS * ROWS
NY = 8
NZ = 8
NX = 4
f32 = jnp.float32
bf16 = jnp.bfloat16
AXES = ("z", "x", "y", "c")


def place():
    return tuple(lax.axis_index(a) for a in AXES)


def remote(src, dst, send, recv, device):
    return pltpu.make_async_remote_copy(
        src_ref=src, dst_ref=dst, send_sem=send, recv_sem=recv, device_id=device, device_id_type=MESH
    )


SUBS = 4
SUB = NBND // SUBS
HALF = NBND // 2
GROUP = 4


def over(a, b, da, db):
    return lax.dot_general(a, b, (((da,), (db,)), ((), ())), preferred_element_type=f32)


def index_kernel(slots, req, out):
    @pl.loop(0, 48)
    def _(i):
        for j in range(8):
            out[NBD + i * 8 + j] = NBD

    @pl.loop(0, TILES)
    def _(t):
        for j in range(NBT):
            s = slots[j, t]
            n = jnp.maximum(s - NBD, 0)
            e = (n * 43) >> 8
            b = jnp.where(s < NBD, s, NBD + e * NBND + req[n - e * CAP, e])
            out[t * NBT + j] = b
            out[NBD + b] = t * NBT + j


def indices(slots, req):
    sm = pl.BlockSpec(memory_space=pltpu.SMEM)
    return pl.pallas_call(
        index_kernel,
        out_shape=jax.ShapeDtypeStruct((512,), jnp.int32),
        in_specs=[sm, sm],
        out_specs=sm,
        name="indices",
    )(slots, req)


def layer_kernel(
    places, boundary, nbr, neg, weight, feat,
    own_out, out, dw_out, loss_out,
    table, cand, ct, cn, xw, aggs, emb, slope, eh, dss, dpres, own, cg, pre,
    msend, mates, rbuf, lbuf, rsend, lsend,
    dw, lossp, w0, sum0, lossb, a1, b1, a2, b2, sum1, sum3, sum2, ybuf, total, ag2a, ag2b, ag1,
    fsem, osem, grs, grr, gls, glr, gcs, gcr, ms, mr, rs, rr, ls, lr, ws, wr,
):
    z, x, y, c = place()
    o = 1 - c
    right = (z, x, lax.rem(y + 1, NY), c)
    left = (z, x, lax.rem(y + NY - 1, NY), c)
    mate = (z, x, y, o)

    def zs(k):
        return (lax.rem(z + k, NZ), x, y, c)

    def xs(k):
        return (z, lax.rem(x + k, NX), y, c)

    def ys(k):
        return (z, x, lax.rem(y + k, NY), c)

    sent = []

    def go(copy):
        copy.start()
        sent.append(copy)
        return copy

    def rows(first, n):
        return pl.ds(pl.multiple_of(first, 8), n)

    def slot(yy, cc):
        return NBD + (lax.rem(yy + NY, NY) * 2 + cc) * NBND

    load = pltpu.make_async_copy(feat, table.at[pl.ds(0, NBD)], fsem)
    load.start()
    load.wait()
    me = slot(y, c)
    for p in range(NBND):
        table[me + p] = table[boundary[p]]
    peers = [mate] + [zs(k) for k in range(1, NZ)] + [xs(k) for k in range(1, NX)] + [ys(k) for k in range(1, NY)]
    barrier = pltpu.get_barrier_semaphore()
    for d in peers:
        pl.semaphore_signal(barrier, inc=1, device_id=d, device_id_type=MESH)

    kio = lax.broadcasted_iota(jnp.int32, (TILE, TILE), 0)
    inv_root = D ** (-0.5)

    def at(t, n=1):
        return pl.ds(pl.multiple_of(t * TILE, TILE), n * TILE)

    def counted(g, _):
        for i in range(2):
            t = g * 2 + i
            nb = nbr[:, at(t)]
            v = jnp.zeros((TILE, TILE), f32)
            for j in range(DEG):
                v += jnp.where(nb[j : j + 1, :] == kio, 1.0, 0.0)
            ct[at(t), :] = v.astype(bf16)
            cn[at(t), :] = v.T.astype(bf16)
        return 0

    lax.fori_loop(0, TILES // 2, counted, 0)
    pl.semaphore_wait(barrier, len(peers))

    def piece(s, q):
        return table.at[pl.ds(s + q * SUB, SUB)]

    def to_right(d, q):
        v = piece(slot(y - d, c), q)
        return remote(v, v, grs.at[d, q], grr.at[d, q], right)

    def from_left(d, q):
        v = piece(slot(y - 1 - d, c), q)
        return remote(v, v, grs.at[d, q], grr.at[d, q], right)

    def to_left(d, q):
        v = piece(slot(y + d, c), q)
        return remote(v, v, gls.at[d, q], glr.at[d, q], left)

    def from_right(d, q):
        v = piece(slot(y + 1 + d, c), q)
        return remote(v, v, gls.at[d, q], glr.at[d, q], left)

    def mate_copy(k, s, q):
        v = piece(s, q)
        return remote(v, v, gcs.at[k, q], gcr.at[k, q], mate)

    half = SUBS // 2
    for q in range(SUBS):
        go(to_right(0, q))
        go(to_left(0, SUBS - 1 - q))
    for q in range(SUBS):
        go(mate_copy(0, me, q))

    def own_part(g):
        v = table[pl.ds(g * GROUP * NBT, GROUP * NBT)].reshape(GROUP * TILE, D)
        xw[at(g * GROUP, GROUP), :] = over(v, weight[:D, :], 1, 0)

    for d in range(1, 5):
        for q in range(SUBS):
            if d < 4 or q < half:
                from_left(d - 1, q).wait_recv()
                if d < 3 or (d == 3 and q < half):
                    go(to_right(d, q))
                go(mate_copy(d, slot(y - d, c), q))
            b = SUBS - 1 - q
            if d < 4 or b >= half:
                from_right(d - 1, b).wait_recv()
                if d < 3 or (d == 3 and b >= half):
                    go(to_left(d, b))
                go(mate_copy(d if d == 4 else 8 - d, slot(y + d, c), b))
            if d < 4 and q == 0:
                own_part(d - 1)
                if d == 3:
                    own_part(3)
    for k in range(8):
        for q in range(SUBS):
            mate_copy(k, slot(y - k, o), q).wait_recv()

    def aggregated(g, _):
        cands = []
        for i in range(GROUP):
            t = g * GROUP + i
            v = jnp.concatenate([table[places[t * NBT + j]] for j in range(NBT)], axis=0)
            cand[at(t), :] = v
            cands.append(v)
        for i in range(GROUP):
            t = g * GROUP + i
            aggs[at(t), :] = (over(cn[at(t), :], cands[i], 1, 0) / DEG).astype(bf16)
        return 0

    def embedded(g, _):
        first = g * GROUP * TILE
        pre[...] = xw[at(g * GROUP, GROUP), :] + over(aggs[at(g * GROUP, GROUP), :], weight[D:, :], 1, 0)
        step = 64
        for r in range(0, GROUP * TILE, step):
            v = pre[r : r + step, :]
            gate = jax.nn.sigmoid(v)
            hid = v * gate
            scale = lax.rsqrt(jnp.mean(hid * hid, axis=-1, keepdims=True) + 1e-06)
            e = hid * scale
            where = pl.ds(pl.multiple_of(first + r, step), step)
            emb[where, :] = e
            eh[where, :] = e.astype(bf16)
            slope[where, :] = scale * (gate * (1.0 + v * (1.0 - gate)))
        return 0

    def scored(g, loss):
        scs = [over(cand[at(g * GROUP + i), :], eh[at(g * GROUP + i), :], 1, 1) * inv_root for i in range(GROUP)]
        for i in range(GROUP):
            t = g * GROUP + i
            sc = scs[i]
            nb = nbr[:, at(t)]
            ng = neg[:, at(t)]
            pos = nb[0:1, :] == kio
            ps = jnp.sum(jnp.where(pos, sc, 0.0), axis=0, keepdims=True)
            negs = [ng[n : n + 1, :] == kio for n in range(NNEG)]
            ns = [jnp.sum(jnp.where(m, sc, 0.0), axis=0, keepdims=True) for m in negs]
            ex = 0.5 + jnp.concatenate(ns, axis=0) - ps
            loss += jax.nn.softplus(ex) * 0.25
            w = jax.nn.sigmoid(ex) * 0.25
            wsum = jnp.sum(w, axis=0, keepdims=True)
            ds = jnp.where(negs[0], w[0:1, :], 0.0)
            for n in range(1, NNEG):
                ds += jnp.where(negs[n], w[n : n + 1, :], 0.0)
            ds = (ds - jnp.where(pos, wsum, 0.0)) * inv_root
            dss[at(t), :] = ds.astype(bf16)
        return loss

    def backed(g, _):
        ds = [over(dss[at(g * GROUP + i), :], cand[at(g * GROUP + i), :], 0, 0) for i in range(GROUP)]
        for i in range(GROUP):
            t = g * GROUP + i
            e = emb[at(t), :]
            m2 = jnp.mean(ds[i] * e, axis=-1, keepdims=True)
            dpres[at(t), :] = (slope[at(t), :] * (ds[i] - e * m2)).astype(bf16)
        return 0

    n = TILES // GROUP
    lax.fori_loop(0, n, aggregated, 0)
    lax.fori_loop(0, n, embedded, 0)
    loss = lax.fori_loop(0, n, scored, jnp.zeros((NNEG, TILE), f32))
    lossp[...] = jnp.broadcast_to(jnp.sum(loss, keepdims=True), (8, 128))
    lax.fori_loop(0, n, backed, 0)

    dp = dpres[...]
    for h in range(2):
        src = table[pl.ds(0, NBD)].reshape(NODES, D) if h == 0 else aggs[...]
        v = over(src, dp, 0, 0)
        for l in range(2):
            dw[l * 512 + h * 256 : l * 512 + h * 256 + 256, :] = v[:, l * 128 : l * 128 + 128]
    first = [
        remote(dw.at[rows(o * 512, 512), :], w0, ws.at[0, 0], wr.at[0, 0], mate),
        remote(lossp, lossb.at[0], ws.at[0, 1], wr.at[0, 1], mate),
    ]
    for copy in first:
        go(copy)

    def returned(g, _):
        di = over(dpres[at(g * GROUP, GROUP), :], weight[...], 1, 1)
        own[pl.ds(g * GROUP * NBT, GROUP * NBT)] = di[:, :D].reshape(GROUP * NBT, BLK, D)
        da = (di[:, D:] / DEG).astype(bf16)
        for i in range(GROUP):
            t = g * GROUP + i
            a = jnp.concatenate([dss[at(t), :], ct[at(t), :]], axis=1)
            b = jnp.concatenate([eh[at(t), :], da[i * TILE : (i + 1) * TILE, :]], axis=0)
            cg[pl.ds(t * NBT, NBT)] = over(a, b, 1, 0).reshape(NBT, BLK, D)
        return 0

    cg[NBD] = jnp.zeros((BLK, D), f32)

    def scatter(stage, src, base, r, buf, n, me, dev):
        buf[me] = src[rows(base + me * r, r), :]
        for k in range(1, n):
            to = lax.rem(me + k, n)
            go(remote(src.at[rows(base + to * r, r), :], buf.at[me], ws.at[stage, k], wr.at[stage, me], dev(k)))

    def arrived(stage, buf, n, me, dev):
        for k in range(1, n):
            who = lax.rem(me + k, n)
            remote(buf.at[who], buf.at[who], ws.at[stage, k], wr.at[stage, who], dev(k)).wait_recv()

    def spread(stage, src, buf, n, me, dev):
        buf[me] = src[...]
        for k in range(1, n):
            go(remote(src, buf.at[me], ws.at[stage, k], wr.at[stage, me], dev(k)))

    def summed(buf, n):
        v = buf[0]
        for i in range(1, n):
            v = v + buf[i]
        return v

    lz, lx, lossz, lossx = lossb.at[pl.ds(2, NZ)], lossb.at[pl.ds(10, NX)], lossb.at[14], lossb.at[15]

    def wa():
        for copy in first:
            copy.wait_recv()
        sum0[...] = dw[rows(c * 512, 512), :] + w0[...]
        lossb[1] = lossp[...] + lossb[0]
        scatter(1, sum0, 0, 32, a1, NZ, z, zs)
        scatter(2, sum0, 256, 64, b1, NX, x, xs)
        spread(3, lossb.at[1], lz, NZ, z, zs)

    def wb():
        arrived(2, b1, NX, x, xs)
        sum1[32:96, :] = summed(b1, NX)
        scatter(4, sum1, 32, 8, b2, NZ, z, zs)

    def wc():
        arrived(1, a1, NZ, z, zs)
        arrived(3, lz, NZ, z, zs)
        sum1[0:32, :] = summed(a1, NZ)
        lossb[14] = summed(lz, NZ)
        scatter(5, sum1, 0, 8, a2, NX, x, xs)
        spread(6, lossz, lx, NX, x, xs)

    def wd():
        arrived(4, b2, NZ, z, zs)
        arrived(5, a2, NX, x, xs)
        arrived(6, lx, NX, x, xs)
        sum2[0:8, :] = summed(a2, NX)
        sum2[8:16, :] = summed(b2, NZ)
        sum2[16:24, :] = summed(lx, NX)
        spread(7, sum2, ybuf, NY, y, ys)

    def we():
        arrived(7, ybuf, NY, y, ys)
        t = summed(ybuf, NY)
        total[...] = t
        loss_out[...] = t[16:24, :]
        spread(8, total.at[pl.ds(0, 8), :], ag2a, NX, x, xs)
        spread(9, total.at[pl.ds(8, 8), :], ag2b, NZ, z, zs)

    def wide(stage, src, r, base, n, me, dev):
        for k in range(1, n):
            go(remote(src, ag1.at[rows(base + me * r, r), :], ws.at[stage, k], wr.at[stage, me], dev(k)))

    def wide_arrived(stage, r, base, n, me, dev):
        for k in range(1, n):
            who = lax.rem(me + k, n)
            v = ag1.at[rows(base + who * r, r), :]
            remote(v, v, ws.at[stage, k], wr.at[stage, who], dev(k)).wait_recv()

    def wf():
        arrived(8, ag2a, NX, x, xs)
        for i in range(NX):
            sum3[i * 8 : i * 8 + 8, :] = ag2a[i]
        wide(10, sum3.at[pl.ds(0, 32), :], 32, 0, NZ, z, zs)
        ag1[rows(z * 32, 32), :] = sum3[0:32, :]

    def wg():
        arrived(9, ag2b, NZ, z, zs)
        for i in range(NZ):
            sum3[32 + i * 8 : 40 + i * 8, :] = ag2b[i]
        wide(11, sum3.at[pl.ds(32, 64), :], 64, 256, NX, x, xs)
        ag1[rows(256 + x * 64, 64), :] = sum3[32:96, :]

    last = []

    def wh():
        wide_arrived(11, 64, 256, NX, x, xs)
        last.append(go(remote(ag1.at[pl.ds(256, 256), :], dw_out.at[rows(c * 512 + 256, 256), :], ws.at[12, 1], wr.at[12, 1], mate)))
        dw_out[rows(c * 512 + 256, 256), :] = ag1[256:512, :]

    def wi():
        wide_arrived(10, 32, 0, NZ, z, zs)
        last.append(go(remote(ag1.at[pl.ds(0, 256), :], dw_out.at[rows(c * 512, 256), :], ws.at[12, 0], wr.at[12, 0], mate)))
        dw_out[rows(c * 512, 256), :] = ag1[0:256, :]


    order = [4, 3, -3, 2, -2, 1, -1, 0]

    def owner(k):
        return lax.rem(y + k + NY, NY)

    def grad_of(k, core, p):
        return cg[places[2 * NBD + (owner(k) * 2 + core) * NBND + p]]

    mcopies = {}

    def to_mate():
        for i, k in enumerate(order):
            for p in range(NBND):
                msend[i, p] = grad_of(k, o, p)
            mcopies[k] = go(remote(msend.at[i], mates.at[i], ms.at[i], mr.at[i], mate))

    ready = set()

    def summed_block(k, p):
        return grad_of(k, c, p) + mates[order.index(k), p]

    def wait_mate(k):
        if k not in ready:
            mcopies[k].wait_recv()
            ready.add(k)

    def hop(to_right, s, h):
        sb, rb, ss, rsm, dev = (rsend, rbuf, rs, rr, right) if to_right else (lsend, lbuf, ls, lr, left)
        view = pl.ds(h * HALF, HALF)
        return remote(sb.at[s, view], rb.at[s, view], ss.at[s, h], rsm.at[s, h], dev)

    def ring(to_right, s, h):
        start = 0 if (h == 0) == to_right else 1
        k = 4 - s if to_right else (-(4 - s) if s else 4)
        wait_mate(k)
        if s > start:
            hop(to_right, s - 1, h).wait_recv()
        for p in range(h * HALF, (h + 1) * HALF):
            v = summed_block(k, p)
            if s > start:
                v = v + (rbuf if to_right else lbuf)[s - 1, p]
            (rsend if to_right else lsend)[s, p] = v
        go(hop(to_right, s, h))

    def ringed(s, h):
        def run():
            ring(True, s, h)
            ring(False, s, 1 - h)

        return run

    def r4():
        wait_mate(0)
        for h in (1, 0):
            hop(True, 3, h).wait_recv()
            hop(False, 3, 1 - h).wait_recv()
        for p in range(NBND):
            out[p] = summed_block(0, p) + rbuf[3, p] + lbuf[3, p]

    results = []

    def own_sum():
        def body(g, _):
            for i in range(8):
                b = g * 8 + i
                own[b] = own[b] + cg[places[NBD + b]]
            return 0

        lax.fori_loop(0, NBD // 8, body, 0)
        copy = pltpu.make_async_copy(own, own_out, osem)
        copy.start()
        results.append(copy)

    lax.fori_loop(0, n // 2, returned, 0)
    wa()
    lax.fori_loop(n // 2, n, returned, 0)
    to_mate()
    for step in (
        ringed(0, 0), ringed(1, 1), wb, own_sum, wc, ringed(1, 0), wd, ringed(2, 1), we, ringed(2, 0),
        ringed(3, 1), wg, wf, ringed(3, 0), wh, wi, r4,
    ):
        step()
    for copy in last:
        copy.wait_recv()
    for copy in sent:
        copy.wait_send()
    for copy in results:
        copy.wait()


def layer(places, boundary, nbr, neg, weight, features):
    vm = pl.BlockSpec(memory_space=pltpu.VMEM)
    sm = pl.BlockSpec(memory_space=pltpu.SMEM)
    hbm = pl.BlockSpec(memory_space=pl.ANY)
    V = pltpu.VMEM
    sem = pltpu.SemaphoreType.DMA
    return pl.pallas_call(
        layer_kernel,
        out_shape=(
            jax.ShapeDtypeStruct((NBD, BLK, D), f32),
            jax.ShapeDtypeStruct((NBND, BLK, D), f32),
            jax.ShapeDtypeStruct((1024, 128), f32),
            jax.ShapeDtypeStruct((8, 128), f32),
        ),
        in_specs=[sm, sm, vm, vm, vm, hbm],
        out_specs=(hbm, vm, vm, vm),
        scratch_shapes=[
            V((TABLE // BLK, BLK, D), bf16),
            V((NODES, D), bf16),
            V((NODES, TILE), bf16),
            V((NODES, TILE), bf16),
            V((NODES, D), f32),
            V((NODES, D), bf16),
            V((NODES, D), f32),
            V((NODES, D), f32),
            V((NODES, D), bf16),
            V((NODES, TILE), bf16),
            V((NODES, D), bf16),
            V((NBD, BLK, D), f32),
            V((NBD + 1, BLK, D), f32),
            V((GROUP * TILE, D), f32),
            V((8, NBND, BLK, D), f32),
            V((8, NBND, BLK, D), f32),
            V((4, NBND, BLK, D), f32),
            V((4, NBND, BLK, D), f32),
            V((4, NBND, BLK, D), f32),
            V((4, NBND, BLK, D), f32),
            V((1024, 128), f32),
            V((8, 128), f32),
            V((512, 128), f32),
            V((512, 128), f32),
            V((16, 8, 128), f32),
            V((NZ, 32, 128), f32),
            V((NX, 64, 128), f32),
            V((NX, 8, 128), f32),
            V((NZ, 8, 128), f32),
            V((96, 128), f32),
            V((96, 128), f32),
            V((24, 128), f32),
            V((NY, 24, 128), f32),
            V((24, 128), f32),
            V((NX, 8, 128), f32),
            V((NZ, 8, 128), f32),
            V((512, 128), f32),
            sem(()),
            sem(()),
            sem((4, SUBS)),
            sem((4, SUBS)),
            sem((4, SUBS)),
            sem((4, SUBS)),
            sem((8, SUBS)),
            sem((8, SUBS)),
            sem((8,)),
            sem((8,)),
            sem((4, 2)),
            sem((4, 2)),
            sem((4, 2)),
            sem((4, 2)),
            sem((13, 8)),
            sem((13, 8)),
        ],
        compiler_params=pltpu.CompilerParams(collective_id=0, has_side_effects=True),
        name="layer",
    )(places, boundary, nbr, neg, weight, features)


def add_kernel(boundary, lossin, got, dwt, own, out, wgrad, loss, buf, sems):
    parts = 4
    n = NBD // parts
    for i in range(parts):
        pltpu.make_async_copy(own.at[pl.ds(i * n, n)], buf.at[pl.ds(i * n, n)], sems.at[i]).start()
    wgrad[:, 0:128] = dwt[0:512, :] / NODES
    wgrad[:, 128:256] = dwt[512:1024, :] / NODES
    loss[0] = lossin[0, 0] / (NODES * 512)
    for i in range(parts):
        pltpu.make_async_copy(own.at[pl.ds(i * n, n)], buf.at[pl.ds(i * n, n)], sems.at[i]).wait()
    for p in range(NBND):
        b = boundary[p]
        buf[b] = buf[b] + got[p]
    for i in range(parts):
        pltpu.make_async_copy(buf.at[pl.ds(i * n, n)], out.at[pl.ds(i * n, n)], sems.at[i]).start()
    for i in range(parts):
        pltpu.make_async_copy(buf.at[pl.ds(i * n, n)], out.at[pl.ds(i * n, n)], sems.at[i]).wait()


def added(boundary, lossin, got, dwt, own):
    hbm = pl.BlockSpec(memory_space=pl.ANY)
    vm = pl.BlockSpec(memory_space=pltpu.VMEM)
    sm = pl.BlockSpec(memory_space=pltpu.SMEM)
    return pl.pallas_call(
        add_kernel,
        out_shape=(
            jax.ShapeDtypeStruct((NBD, BLK, D), f32),
            jax.ShapeDtypeStruct((512, 256), f32),
            jax.ShapeDtypeStruct((1,), f32),
        ),
        in_specs=[sm, sm, vm, vm, hbm],
        out_specs=(hbm, vm, sm),
        scratch_shapes=[pltpu.VMEM((NBD, BLK, D), f32), pltpu.SemaphoreType.DMA((4,))],
        name="add_returned",
    )(boundary, lossin, got, dwt, own)


def per_device(features, boundary, request, tile_slots, neighbors, negatives, layer_weight):
    places = indices(tile_slots.T, request.T)
    own, got, dwt, losst = layer(
        places, boundary, neighbors.T, negatives.T, layer_weight, features.reshape(NBD, BLK, D)
    )
    grad, wgrad, loss = added(boundary, losst, got, dwt, own)
    return grad.reshape(NODES, D), wgrad, loss.reshape(())


def solution(mesh):
    finer = Mesh(mesh.devices.reshape(NZ, NX, NY, 2), AXES)
    dg = AXES
    return jax.shard_map(
        per_device,
        mesh=finer,
        in_specs=(P(dg, None), P(dg), P(dg, None), P(dg, None), P(dg, None), P(dg, None), P()),
        out_specs=(P(dg, None), P(), P()),
        check_vma=False,
    )
```

time: 107 us -> 82.1 us (0.77)
  Pallas kernels: 103 us -> 81.2 us
  between operations: 2.47 us -> 0.65 us
  local copies, waits for them, and re-layouts: 1.23 us -> 0 us
    pallas_call x4 -> x3, Pallas kernels: 103 us -> 81.2 us  [the longest x1 73.5 us: layer(): pl.pallas_call(layer_kernel, out_shape=(jax.ShapeDtypeStruct((NBD, BLK, D...]
    slice x2 -> x0, local copies, waits for them, and re-layouts: 1.23 us -> none  [the longest x1 1.19 us: per_device(): return (grad, wgrad, losst[0, 0] / (NODES * 512))]
where the time goes in v2:
time: 82.1 us; the launch traced here: 81.8 us
  Pallas kernels  81.2 us (99%)
    pallas_call x1, Pallas kernels, layer(): pl.pallas_call(layer_kernel, out_shape=(jax.ShapeDtypeStruct((NBD, BLK, D...  73.5 us
    pallas_call x1, Pallas kernels, added(): pl.pallas_call(add_kernel, out_shape=(jax.ShapeDtypeStruct((NBD, BLK, D),...  4.84 us
    pallas_call x1, Pallas kernels, indices(): pl.pallas_call(index_kernel, out_shape=jax.ShapeDtypeStruct((512,), jnp.i...  2.83 us

profile of v2, /device:TPU:1, one launch (start us, length us, event | category | flops | bytes accessed | tf_op | source)
XLA Modules:
  0.0 81.8 jit_solution(202080273626987786)
XLA Ops:
  0.6 2.8 %indices.1.places = s32[512]{0:T(512)} custom-call(s32[8,16]{1,0:T(8,128)} %bitcast.10, s32[6,16]{1,0:T(8,128)} %bitcast.11), custom_call_target="tpu_custom_call" | custom-call | tf_op jit(solution)/shard_map/indices/pallas_call | solution.py:73
  3.5 73.5 %layer.1 = (f32[128,16,256]{2,1,0:T(8,128)}, f32[16,16,256]{2,1,0:T(8,128)}, f32[1024,128]{1,0:T(8,128)}, f32[8,128]{1,0:T(8,128)}) custom-call(s32[512]{0:T(512)} %indices.1.places, s32[16]{0:T(128)} %boundary.3, s32[10,2048]{1,0:T(8,128)} %bitcast.8, s32[4,2048]{1,0:T(4,128)} %bitcast.9, bf16[512,256]{1,0:T(8,128)(2,1)} %weight.1, ...), custom_call_target="tpu_custom_call" | custom-call | tf_op jit(solution)/shard_map/layer/pallas_call | solution.py:492
  77.0 4.8 %add_returned.1 = (f32[128,16,256]{2,1,0:T(8,128)}, f32[512,256]{1,0:T(8,128)}, f32[1]{0:T(128)}) custom-call(s32[16]{0:T(128)} %boundary.3, f32[8,128]{1,0:T(8,128)} %get-tuple-element.10.lossin, f32[16,16,256]{2,1,0:T(8,128)} %get-tuple-element.11.got, f32[1024,128]{1,0:T(8,128)} %get-tuple-element.12.dwt, f32[128,16,256]{2,1,0:T(8,128)} %get-tuple-element.13.own), custom_call_target="tpu_custom_call" | custom-call | tf_op jit(solution)/shard_map/add_returned/pallas_call | solution.py:585

commit v3 on v2

--- a/solution.py
+++ b/solution.py
@@ -51,41 +51,13 @@
     return lax.dot_general(a, b, (((da,), (db,)), ((), ())), preferred_element_type=f32)
 
 
-def index_kernel(slots, req, out):
-    @pl.loop(0, 48)
-    def _(i):
-        for j in range(8):
-            out[NBD + i * 8 + j] = NBD
-
-    @pl.loop(0, TILES)
-    def _(t):
-        for j in range(NBT):
-            s = slots[j, t]
-            n = jnp.maximum(s - NBD, 0)
-            e = (n * 43) >> 8
-            b = jnp.where(s < NBD, s, NBD + e * NBND + req[n - e * CAP, e])
-            out[t * NBT + j] = b
-            out[NBD + b] = t * NBT + j
-
-
-def indices(slots, req):
-    sm = pl.BlockSpec(memory_space=pltpu.SMEM)
-    return pl.pallas_call(
-        index_kernel,
-        out_shape=jax.ShapeDtypeStruct((512,), jnp.int32),
-        in_specs=[sm, sm],
-        out_specs=sm,
-        name="indices",
-    )(slots, req)
-
-
 def layer_kernel(
-    places, boundary, nbr, neg, weight, feat,
-    own_out, out, dw_out, loss_out,
-    table, cand, ct, cn, xw, aggs, emb, slope, eh, dss, dpres, own, cg, pre,
+    slots, req, boundary, nbr, neg, weight, feat,
+    own, out, dw_out, loss_out,
+    table, pack, places, invv, inv, cand, ct, cn, xw, aggs, emb, slope, eh, dss, wn, dpres, cg, pre,
     msend, mates, rbuf, lbuf, rsend, lsend,
     dw, lossp, w0, sum0, lossb, a1, b1, a2, b2, sum1, sum3, sum2, ybuf, total, ag2a, ag2b, ag1,
-    fsem, osem, grs, grr, gls, glr, gcs, gcr, ms, mr, rs, rr, ls, lr, ws, wr,
+    fsem, psem, isem, grs, grr, gls, glr, gcs, gcr, ms, mr, rs, rr, ls, lr, ws, wr,
 ):
     z, x, y, c = place()
     o = 1 - c
@@ -115,22 +87,23 @@
     def slot(yy, cc):
         return NBD + (lax.rem(yy + NY, NY) * 2 + cc) * NBND
 
-    load = pltpu.make_async_copy(feat, table.at[pl.ds(0, NBD)], fsem)
-    load.start()
-    load.wait()
-    me = slot(y, c)
-    for p in range(NBND):
-        table[me + p] = table[boundary[p]]
     peers = [mate] + [zs(k) for k in range(1, NZ)] + [xs(k) for k in range(1, NX)] + [ys(k) for k in range(1, NY)]
     barrier = pltpu.get_barrier_semaphore()
     for d in peers:
         pl.semaphore_signal(barrier, inc=1, device_id=d, device_id_type=MESH)
+    loads = [
+        pltpu.make_async_copy(feat, pack, psem),
+        pltpu.make_async_copy(feat, table.at[pl.ds(0, NBD)], fsem),
+    ]
+    for copy in loads:
+        copy.start()
+    me = slot(y, c)
 
     kio = lax.broadcasted_iota(jnp.int32, (TILE, TILE), 0)
     inv_root = D ** (-0.5)
 
     def at(t, n=1):
-        return pl.ds(pl.multiple_of(t * TILE, TILE), n * TILE)
+        return pl.ds(t * TILE if isinstance(t, int) else pl.multiple_of(t * TILE, TILE), n * TILE)
 
     def counted(g, _):
         for i in range(2):
@@ -144,6 +117,9 @@
         return 0
 
     lax.fori_loop(0, TILES // 2, counted, 0)
+    loads[0].wait()
+    for p in range(NBND):
+        table[me + p] = pack[boundary[p]]
     pl.semaphore_wait(barrier, len(peers))
 
     def piece(s, q):
@@ -175,6 +151,23 @@
         go(to_left(0, SUBS - 1 - q))
     for q in range(SUBS):
         go(mate_copy(0, me, q))
+
+    spot = lax.broadcasted_iota(jnp.int32, (8, 128), 0) * 128 + lax.broadcasted_iota(jnp.int32, (8, 128), 1)
+
+    def placed(t, back):
+        for j in range(NBT):
+            s = slots[j, t]
+            n = jnp.maximum(s - NBD, 0)
+            e = (n * 43) >> 8
+            b = jnp.where(s < NBD, s, NBD + e * NBND + req[n - e * CAP, e])
+            places[t * NBT + j] = b
+            back = jnp.where(spot == b, t * NBT + j, back)
+        return back
+
+    invv[...] = lax.fori_loop(0, TILES, placed, jnp.full((8, 128), NBD, jnp.int32))
+    down = pltpu.make_async_copy(invv, inv, isem)
+    down.start()
+    loads[1].wait()
 
     def own_part(g):
         v = table[pl.ds(g * GROUP * NBT, GROUP * NBT)].reshape(GROUP * TILE, D)
@@ -201,6 +194,8 @@
         for q in range(SUBS):
             mate_copy(k, slot(y - k, o), q).wait_recv()
 
+    down.wait()
+
     def aggregated(g, _):
         cands = []
         for i in range(GROUP):
@@ -215,15 +210,15 @@
 
     def embedded(g, _):
         first = g * GROUP * TILE
-        pre[...] = xw[at(g * GROUP, GROUP), :] + over(aggs[at(g * GROUP, GROUP), :], weight[D:, :], 1, 0)
-        step = 64
+        pre[g % 2] = xw[at(g * GROUP, GROUP), :] + over(aggs[at(g * GROUP, GROUP), :], weight[D:, :], 1, 0)
+        step = 32
         for r in range(0, GROUP * TILE, step):
-            v = pre[r : r + step, :]
+            v = pre[g % 2, r : r + step, :]
             gate = jax.nn.sigmoid(v)
             hid = v * gate
             scale = lax.rsqrt(jnp.mean(hid * hid, axis=-1, keepdims=True) + 1e-06)
             e = hid * scale
-            where = pl.ds(pl.multiple_of(first + r, step), step)
+            where = pl.ds(first + r, step)
             emb[where, :] = e
             eh[where, :] = e.astype(bf16)
             slope[where, :] = scale * (gate * (1.0 + v * (1.0 - gate)))
@@ -236,22 +231,22 @@
             sc = scs[i]
             nb = nbr[:, at(t)]
             ng = neg[:, at(t)]
-            pos = nb[0:1, :] == kio
-            ps = jnp.sum(jnp.where(pos, sc, 0.0), axis=0, keepdims=True)
-            negs = [ng[n : n + 1, :] == kio for n in range(NNEG)]
-            ns = [jnp.sum(jnp.where(m, sc, 0.0), axis=0, keepdims=True) for m in negs]
+            ps = jnp.sum(jnp.where(nb[0:1, :] == kio, sc, 0.0), axis=0, keepdims=True)
+            ns = [jnp.sum(jnp.where(ng[n : n + 1, :] == kio, sc, 0.0), axis=0, keepdims=True) for n in range(NNEG)]
             ex = 0.5 + jnp.concatenate(ns, axis=0) - ps
             loss += jax.nn.softplus(ex) * 0.25
             w = jax.nn.sigmoid(ex) * 0.25
-            wsum = jnp.sum(w, axis=0, keepdims=True)
-            ds = jnp.where(negs[0], w[0:1, :], 0.0)
-            for n in range(1, NNEG):
-                ds += jnp.where(negs[n], w[n : n + 1, :], 0.0)
-            ds = (ds - jnp.where(pos, wsum, 0.0)) * inv_root
-            dss[at(t), :] = ds.astype(bf16)
+            wn[t] = jnp.concatenate([w, jnp.sum(w, axis=0, keepdims=True), jnp.zeros((3, TILE), f32)], axis=0)
         return loss
 
     def backed(g, _):
+        for i in range(GROUP):
+            t = g * GROUP + i
+            ng = neg[:, at(t)]
+            v = jnp.where(nbr[0:1, at(t)] == kio, -wn[t, 4:5, :], 0.0)
+            for n in range(NNEG):
+                v += jnp.where(ng[n : n + 1, :] == kio, wn[t, n : n + 1, :], 0.0)
+            dss[at(t), :] = (v * inv_root).astype(bf16)
         ds = [over(dss[at(g * GROUP + i), :], cand[at(g * GROUP + i), :], 0, 0) for i in range(GROUP)]
         for i in range(GROUP):
             t = g * GROUP + i
@@ -261,11 +256,17 @@
         return 0
 
     n = TILES // GROUP
-    lax.fori_loop(0, n, aggregated, 0)
-    lax.fori_loop(0, n, embedded, 0)
-    loss = lax.fori_loop(0, n, scored, jnp.zeros((NNEG, TILE), f32))
+    loss = jnp.zeros((NNEG, TILE), f32)
+    for step in range(n + 3):
+        if step >= 3:
+            backed(step - 3, 0)
+        if 2 <= step < n + 2:
+            loss = scored(step - 2, loss)
+        if 1 <= step < n + 1:
+            embedded(step - 1, 0)
+        if step < n:
+            aggregated(step, 0)
     lossp[...] = jnp.broadcast_to(jnp.sum(loss, keepdims=True), (8, 128))
-    lax.fori_loop(0, n, backed, 0)
 
     dp = dpres[...]
     for h in range(2):
@@ -293,9 +294,12 @@
 
     cg[NBD] = jnp.zeros((BLK, D), f32)
 
+    def others(n):
+        return sorted(range(1, n), key=lambda k: -min(k, n - k))
+
     def scatter(stage, src, base, r, buf, n, me, dev):
         buf[me] = src[rows(base + me * r, r), :]
-        for k in range(1, n):
+        for k in others(n):
             to = lax.rem(me + k, n)
             go(remote(src.at[rows(base + to * r, r), :], buf.at[me], ws.at[stage, k], wr.at[stage, me], dev(k)))
 
@@ -306,7 +310,7 @@
 
     def spread(stage, src, buf, n, me, dev):
         buf[me] = src[...]
-        for k in range(1, n):
+        for k in others(n):
             go(remote(src, buf.at[me], ws.at[stage, k], wr.at[stage, me], dev(k)))
 
     def summed(buf, n):
@@ -357,7 +361,7 @@
         spread(9, total.at[pl.ds(8, 8), :], ag2b, NZ, z, zs)
 
     def wide(stage, src, r, base, n, me, dev):
-        for k in range(1, n):
+        for k in others(n):
             go(remote(src, ag1.at[rows(base + me * r, r), :], ws.at[stage, k], wr.at[stage, me], dev(k)))
 
     def wide_arrived(stage, r, base, n, me, dev):
@@ -399,7 +403,8 @@
         return lax.rem(y + k + NY, NY)
 
     def grad_of(k, core, p):
-        return cg[places[2 * NBD + (owner(k) * 2 + core) * NBND + p]]
+        q = (owner(k) * 2 + core) * NBND + p
+        return cg[inv[1 + q // 128, q % 128]]
 
     mcopies = {}
 
@@ -452,19 +457,14 @@
         for p in range(NBND):
             out[p] = summed_block(0, p) + rbuf[3, p] + lbuf[3, p]
 
-    results = []
-
     def own_sum():
         def body(g, _):
             for i in range(8):
                 b = g * 8 + i
-                own[b] = own[b] + cg[places[NBD + b]]
+                own[b] = own[b] + cg[inv[0, b]]
             return 0
 
         lax.fori_loop(0, NBD // 8, body, 0)
-        copy = pltpu.make_async_copy(own, own_out, osem)
-        copy.start()
-        results.append(copy)
 
     lax.fori_loop(0, n // 2, returned, 0)
     wa()
@@ -479,11 +479,9 @@
         copy.wait_recv()
     for copy in sent:
         copy.wait_send()
-    for copy in results:
-        copy.wait()
-
-
-def layer(places, boundary, nbr, neg, weight, features):
+
+
+def layer(slots, req, boundary, nbr, neg, weight, features):
     vm = pl.BlockSpec(memory_space=pltpu.VMEM)
     sm = pl.BlockSpec(memory_space=pltpu.SMEM)
     hbm = pl.BlockSpec(memory_space=pl.ANY)
@@ -492,15 +490,19 @@
     return pl.pallas_call(
         layer_kernel,
         out_shape=(
-            jax.ShapeDtypeStruct((NBD, BLK, D), f32),
-            jax.ShapeDtypeStruct((NBND, BLK, D), f32),
-            jax.ShapeDtypeStruct((1024, 128), f32),
+            pltpu.VMEM((NBD, BLK, D), f32),
+            pltpu.VMEM((NBND, BLK, D), f32),
+            pltpu.VMEM((1024, 128), f32),
             jax.ShapeDtypeStruct((8, 128), f32),
         ),
-        in_specs=[sm, sm, vm, vm, vm, hbm],
-        out_specs=(hbm, vm, vm, vm),
+        in_specs=[sm, sm, sm, vm, vm, vm, hbm],
+        out_specs=(vm, vm, vm, vm),
         scratch_shapes=[
             V((TABLE // BLK, BLK, D), bf16),
+            V((NBD, BLK, D), bf16),
+            pltpu.SMEM((NBD,), jnp.int32),
+            V((8, 128), jnp.int32),
+            pltpu.SMEM((8, 128), jnp.int32),
             V((NODES, D), bf16),
             V((NODES, TILE), bf16),
             V((NODES, TILE), bf16),
@@ -510,10 +512,10 @@
             V((NODES, D), f32),
             V((NODES, D), bf16),
             V((NODES, TILE), bf16),
+            V((TILES, 8, TILE), f32),
             V((NODES, D), bf16),
-            V((NBD, BLK, D), f32),
             V((NBD + 1, BLK, D), f32),
-            V((GROUP * TILE, D), f32),
+            V((2, GROUP * TILE, D), f32),
             V((8, NBND, BLK, D), f32),
             V((8, NBND, BLK, D), f32),
             V((4, NBND, BLK, D), f32),
@@ -539,6 +541,7 @@
             V((512, 128), f32),
             sem(()),
             sem(()),
+            sem(()),
             sem((4, SUBS)),
             sem((4, SUBS)),
             sem((4, SUBS)),
@@ -556,32 +559,36 @@
         ],
         compiler_params=pltpu.CompilerParams(collective_id=0, has_side_effects=True),
         name="layer",
-    )(places, boundary, nbr, neg, weight, features)
-
-
-def add_kernel(boundary, lossin, got, dwt, own, out, wgrad, loss, buf, sems):
+    )(slots, req, boundary, nbr, neg, weight, features)
+
+
+def add_kernel(boundary, lossin, got, dwt, own, out, wgrad, loss, buf, wg, sems):
     parts = 4
     n = NBD // parts
-    for i in range(parts):
-        pltpu.make_async_copy(own.at[pl.ds(i * n, n)], buf.at[pl.ds(i * n, n)], sems.at[i]).start()
-    wgrad[:, 0:128] = dwt[0:512, :] / NODES
-    wgrad[:, 128:256] = dwt[512:1024, :] / NODES
-    loss[0] = lossin[0, 0] / (NODES * 512)
-    for i in range(parts):
-        pltpu.make_async_copy(own.at[pl.ds(i * n, n)], buf.at[pl.ds(i * n, n)], sems.at[i]).wait()
+    @pl.loop(0, 16)
+    def _(i):
+        buf[pl.ds(i * 8, 8)] = own[pl.ds(i * 8, 8)]
+
     for p in range(NBND):
         b = boundary[p]
         buf[b] = buf[b] + got[p]
-    for i in range(parts):
-        pltpu.make_async_copy(buf.at[pl.ds(i * n, n)], out.at[pl.ds(i * n, n)], sems.at[i]).start()
-    for i in range(parts):
-        pltpu.make_async_copy(buf.at[pl.ds(i * n, n)], out.at[pl.ds(i * n, n)], sems.at[i]).wait()
+    outs = [pltpu.make_async_copy(buf.at[pl.ds(i * n, n)], out.at[pl.ds(i * n, n)], sems.at[i]) for i in range(parts)]
+    for copy in outs:
+        copy.start()
+    loss[0] = lossin[0, 0] / (NODES * 512)
+    wg[:, 0:128] = dwt[0:512, :] / NODES
+    wg[:, 128:256] = dwt[512:1024, :] / NODES
+    outs.append(pltpu.make_async_copy(wg, wgrad, sems.at[parts]))
+    outs[-1].start()
+    for copy in outs:
+        copy.wait()
 
 
 def added(boundary, lossin, got, dwt, own):
     hbm = pl.BlockSpec(memory_space=pl.ANY)
+    sm = pl.BlockSpec(memory_space=pltpu.SMEM)
     vm = pl.BlockSpec(memory_space=pltpu.VMEM)
-    sm = pl.BlockSpec(memory_space=pltpu.SMEM)
+    here = [pltpu.with_memory_space_constraint(v, pltpu.VMEM) for v in (got, dwt, own)]
     return pl.pallas_call(
         add_kernel,
         out_shape=(
@@ -589,17 +596,20 @@
             jax.ShapeDtypeStruct((512, 256), f32),
             jax.ShapeDtypeStruct((1,), f32),
         ),
-        in_specs=[sm, sm, vm, vm, hbm],
-        out_specs=(hbm, vm, sm),
-        scratch_shapes=[pltpu.VMEM((NBD, BLK, D), f32), pltpu.SemaphoreType.DMA((4,))],
+        in_specs=[sm, sm, vm, vm, vm],
+        out_specs=(hbm, hbm, sm),
+        scratch_shapes=[
+            pltpu.VMEM((NBD, BLK, D), f32),
+            pltpu.VMEM((512, 256), f32),
+            pltpu.SemaphoreType.DMA((6,)),
+        ],
         name="add_returned",
-    )(boundary, lossin, got, dwt, own)
+    )(boundary, lossin, *here)
 
 
 def per_device(features, boundary, request, tile_slots, neighbors, negatives, layer_weight):
-    places = indices(tile_slots.T, request.T)
     own, got, dwt, losst = layer(
-        places, boundary, neighbors.T, negatives.T, layer_weight, features.reshape(NBD, BLK, D)
+        tile_slots.T, request.T, boundary, neighbors.T, negatives.T, layer_weight, features.reshape(NBD, BLK, D)
     )
     grad, wgrad, loss = added(boundary, losst, got, dwt, own)
     return grad.reshape(NODES, D), wgrad, loss.reshape(())

time: 82.1 us -> 72.3 us (0.88)
  Pallas kernels: 81.2 us -> 71.5 us
    pallas_call x2 -> x1, Pallas kernels: 76.3 us -> 68.5 us  [layer(): pl.pallas_call(layer_kernel, out_shape=(pltpu.VMEM((NBD, BLK, D), f32), p...]
    pallas_call x1, Pallas kernels: 4.84 us -> 3.03 us  [added(): pl.pallas_call(add_kernel, out_shape=(jax.ShapeDtypeStruct((NBD, BLK, D),...]
where the time goes in v3:
time: 72.3 us; the launch traced here: 72.1 us
  Pallas kernels  71.5 us (99%)
    pallas_call x1, Pallas kernels, layer(): pl.pallas_call(layer_kernel, out_shape=(pltpu.VMEM((NBD, BLK, D), f32), p...  68.5 us
    pallas_call x1, Pallas kernels, added(): pl.pallas_call(add_kernel, out_shape=(jax.ShapeDtypeStruct((NBD, BLK, D),...  3.03 us

profile of v3, /device:TPU:1, one launch (start us, length us, event | category | flops | bytes accessed | tf_op | source)
XLA Modules:
  0.0 72.1 jit_solution(16759552958035386608)
XLA Ops:
  0.6 68.5 %layer.1 = (f32[128,16,256]{2,1,0:T(8,128)S(1)}, f32[16,16,256]{2,1,0:T(8,128)S(1)}, f32[1024,128]{1,0:T(8,128)S(1)}, f32[8,128]{1,0:T(8,128)}) custom-call(s32[8,16]{1,0:T(8,128)} %bitcast.10, s32[6,16]{1,0:T(8,128)} %bitcast.11, s32[16]{0:T(128)} %boundary.3, s32[10,2048]{1,0:T(8,128)} %bitcast.8, s32[4,2048]{1,0:T(4,128)} %bitcast.9, ...), custom_call_target="tpu_custom_call" | custom-call | tf_op jit(solution)/shard_map/layer/pallas_call | solution.py:490
  69.1 3.0 %add_returned.1 = (f32[128,16,256]{2,1,0:T(8,128)}, f32[512,256]{1,0:T(8,128)}, f32[1]{0:T(128)}) custom-call(s32[16]{0:T(128)} %boundary.3, f32[8,128]{1,0:T(8,128)} %get-tuple-element.10.lossin, f32[16,16,256]{2,1,0:T(8,128)S(1)} %get-tuple-element.11.got, f32[1024,128]{1,0:T(8,128)S(1)} %get-tuple-element.12.dwt, f32[128,16,256]{2,1,0:T(8,128)S(1)} %get-tuple-element.13.own), custom_call_target="tpu_custom_call" | custom-call | tf_op jit(solution)/shard_map/add_returned/pallas_call | solution.py:592

commit v4 on v3

--- a/solution.py
+++ b/solution.py
@@ -116,7 +116,6 @@
             cn[at(t), :] = v.T.astype(bf16)
         return 0
 
-    lax.fori_loop(0, TILES // 2, counted, 0)
     loads[0].wait()
     for p in range(NBND):
         table[me + p] = pack[boundary[p]]
@@ -173,6 +172,11 @@
         v = table[pl.ds(g * GROUP * NBT, GROUP * NBT)].reshape(GROUP * TILE, D)
         xw[at(g * GROUP, GROUP), :] = over(v, weight[:D, :], 1, 0)
 
+    for g in range(2):
+        counted(g, 0)
+    chores = [functools.partial(counted, g, 0) for g in range(2, 5)]
+    chores += [functools.partial(own_part, g) for g in range(4)]
+    chores += [functools.partial(counted, g, 0) for g in range(5, 8)]
     for d in range(1, 5):
         for q in range(SUBS):
             if d < 4 or q < half:
@@ -186,10 +190,8 @@
                 if d < 3 or (d == 3 and b >= half):
                     go(to_left(d, b))
                 go(mate_copy(d if d == 4 else 8 - d, slot(y + d, c), b))
-            if d < 4 and q == 0:
-                own_part(d - 1)
-                if d == 3:
-                    own_part(3)
+            if chores:
+                chores.pop(0)()
     for k in range(8):
         for q in range(SUBS):
             mate_copy(k, slot(y - k, o), q).wait_recv()
@@ -255,10 +257,24 @@
             dpres[at(t), :] = (slope[at(t), :] * (ds[i] - e * m2)).astype(bf16)
         return 0
 
+    def weighed(g):
+        dp = dpres[at(g * GROUP, GROUP), :]
+        for h in range(2):
+            src = aggs[at(g * GROUP, GROUP), :]
+            if h == 0:
+                src = table[pl.ds(g * GROUP * NBT, GROUP * NBT)].reshape(GROUP * TILE, D)
+            v = over(src, dp, 0, 0)
+            for l in range(2):
+                where = slice(l * 512 + h * 256, l * 512 + h * 256 + 256)
+                part = v[:, l * 128 : l * 128 + 128]
+                dw[where, :] = part if g == 0 else dw[where, :] + part
+
     n = TILES // GROUP
     loss = jnp.zeros((NNEG, TILE), f32)
-    for step in range(n + 3):
-        if step >= 3:
+    for step in range(n + 4):
+        if step >= 4:
+            weighed(step - 4)
+        if 3 <= step < n + 3:
             backed(step - 3, 0)
         if 2 <= step < n + 2:
             loss = scored(step - 2, loss)
@@ -268,12 +284,6 @@
             aggregated(step, 0)
     lossp[...] = jnp.broadcast_to(jnp.sum(loss, keepdims=True), (8, 128))
 
-    dp = dpres[...]
-    for h in range(2):
-        src = table[pl.ds(0, NBD)].reshape(NODES, D) if h == 0 else aggs[...]
-        v = over(src, dp, 0, 0)
-        for l in range(2):
-            dw[l * 512 + h * 256 : l * 512 + h * 256 + 256, :] = v[:, l * 128 : l * 128 + 128]
     first = [
         remote(dw.at[rows(o * 512, 512), :], w0, ws.at[0, 0], wr.at[0, 0], mate),
         remote(lossp, lossb.at[0], ws.at[0, 1], wr.at[0, 1], mate),
@@ -471,8 +481,8 @@
     lax.fori_loop(n // 2, n, returned, 0)
     to_mate()
     for step in (
-        ringed(0, 0), ringed(1, 1), wb, own_sum, wc, ringed(1, 0), wd, ringed(2, 1), we, ringed(2, 0),
-        ringed(3, 1), wg, wf, ringed(3, 0), wh, wi, r4,
+        ringed(0, 0), ringed(1, 1), wb, own_sum, wc, ringed(1, 0), wd, ringed(2, 1), ringed(2, 0), we, ringed(3, 1),
+        wf, wg, ringed(3, 0), wh, wi, r4,
     ):
         step()
     for copy in last:

time: 72.3 us -> 71.8 us (level)
  no operation moved by 1% of the time
where the time goes in v4:
time: 71.8 us; the launch traced here: 71.6 us
  Pallas kernels  70.9 us (99%)
    pallas_call x1, Pallas kernels, layer(): pl.pallas_call(layer_kernel, out_shape=(pltpu.VMEM((NBD, BLK, D), f32), p...  67.9 us
    pallas_call x1, Pallas kernels, added(): pl.pallas_call(add_kernel, out_shape=(jax.ShapeDtypeStruct((NBD, BLK, D),...  3.03 us

profile of v4, /device:TPU:1, one launch (start us, length us, event | category | flops | bytes accessed | tf_op | source)
XLA Modules:
  0.0 71.6 jit_solution(4382388303979946365)
XLA Ops:
  0.6 67.9 %layer.1 = (f32[128,16,256]{2,1,0:T(8,128)S(1)}, f32[16,16,256]{2,1,0:T(8,128)S(1)}, f32[1024,128]{1,0:T(8,128)S(1)}, f32[8,128]{1,0:T(8,128)}) custom-call(s32[8,16]{1,0:T(8,128)} %bitcast.10, s32[6,16]{1,0:T(8,128)} %bitcast.11, s32[16]{0:T(128)} %boundary.3, s32[10,2048]{1,0:T(8,128)} %bitcast.8, s32[4,2048]{1,0:T(4,128)} %bitcast.9, ...), custom_call_target="tpu_custom_call" | custom-call | tf_op jit(solution)/shard_map/layer/pallas_call | solution.py:500
  68.5 3.0 %add_returned.1 = (f32[128,16,256]{2,1,0:T(8,128)}, f32[512,256]{1,0:T(8,128)}, f32[1]{0:T(128)}) custom-call(s32[16]{0:T(128)} %boundary.3, f32[8,128]{1,0:T(8,128)} %get-tuple-element.10.lossin, f32[16,16,256]{2,1,0:T(8,128)S(1)} %get-tuple-element.11.got, f32[1024,128]{1,0:T(8,128)S(1)} %get-tuple-element.12.dwt, f32[128,16,256]{2,1,0:T(8,128)S(1)} %get-tuple-element.13.own), custom_call_target="tpu_custom_call" | custom-call | tf_op jit(solution)/shard_map/add_returned/pallas_call | solution.py:602
